TPU v7x, 512 devices: a whole 4x4x16 slice. The times are simulated.
512 devices in a mesh: ev: 8 (over y_hi, x), sp: 64 (over z, y_lo, core).
Axes of the slice: x: 4, y: 4 (y_hi: 2, y_lo: 2; y = y_hi * 2 + y_lo), z: 16, core: 2. Of those that a mesh axis runs over, the one named last changes fastest.
Arguments:
- partial_kernels: float32 [8, 32, 512, 128], P('ev', None, 'sp'), may hold values from -6 to 6
- block_ids: int32 [8, 512], P('ev', 'sp'), may hold values from 0 to 255, as said below
- radial_smoother: float32 [128, 128], replicated, may hold values from -0.5 to 2
- shell_level: int32 [128], P('sp'), may hold values from 1 to 4
- lateral_scale: float32 [512, 1024], replicated, may hold values from 0.5 to 1
Outputs:
- smoothed_kernel: float32 [128, 512, 1024], P('sp', None, 'ev')
Inputs may be any that keep to these rules, and one draw needn't show every extreme that they name: `block_ids`: each index of ev and sp holds 8 distinct ids; an id's owner is id // 32; one holder gives at most 2 ids to one owner, and in every stripe some owner receives 2 ids from every group.
All inputs are finite; a program needn't handle non-finite values.
Results may differ from a plain program's by a relative error of at most 0.000073.
Values sent between devices are 32-bit elements; how exact they have to be, the bound alone decides.
No kernel may reach another device: no remote copies, remote signals or barrier semaphores. Data moves between devices by JAX's collectives and lax.ppermute only.
A program may use at most 64 MiB of HBM per device.

v0:
```python
import jax
import jax.numpy as jnp
from jax import lax
from jax.sharding import PartitionSpec as P

NR = 128
BPT = 8
CAP = 2
PASSES = 4
NSEG = 4


diffusion_rate = 0.0615


def padded_2(cells, sides, width):
    for axis, dim in sides:
        count = lax.axis_size(axis)
        ends = count - 1
        head = lax.slice_in_dim(cells, 0, width, axis=dim)
        tail = lax.slice_in_dim(cells, cells.shape[dim] - width, cells.shape[dim], axis=dim)
        cells = jnp.concatenate(
            [
                lax.ppermute(tail, axis, [(i, (i + 1) % count) for i in range(ends)]),
                cells,
                lax.ppermute(head, axis, [((i + 1) % count, i) for i in range(ends)]),
            ],
            axis=dim,
        )
    return cells


def per_device(partial_kernels, block_ids, radial_smoother, shell_level, lateral_scale):
    groups = lax.axis_size("ev")
    per_owner = BPT * NSEG
    blocks = partial_kernels[0]
    block_list = block_ids[0]
    owners = block_list // per_owner
    within = block_list % per_owner
    listed = block_list.shape[0]
    same_owner = owners[:, None] == owners[None, :]
    earlier = jnp.arange(listed)[None, :] < jnp.arange(listed)[:, None]
    ranking = jnp.sum(same_owner & earlier, axis=1)
    slot_of = owners * CAP + ranking
    placing = (slot_of[None, :] == jnp.arange(groups * CAP, dtype=jnp.int32)[:, None]).astype(
        jnp.float32
    )
    packed = jnp.einsum("rjc,sj->rsc", blocks, placing, precision=lax.Precision.HIGHEST)
    label_out = (
        jnp.dot(placing, within.astype(jnp.float32) + 1.0, precision=lax.Precision.HIGHEST) - 1.0
    )
    label_out = label_out.reshape(1, groups * CAP, 1)
    arrived, labels = (
        lax.all_to_all(packed, "ev", split_axis=1, concat_axis=1, tiled=True),
        lax.all_to_all(label_out, "ev", split_axis=1, concat_axis=1, tiled=True),
    )
    picker = (labels.reshape(1, -1) == jnp.arange(per_owner, dtype=jnp.float32)[:, None]).astype(
        jnp.float32
    )
    column_tile = jnp.einsum("rsc,ls->lrc", arrived, picker, precision=lax.Precision.HIGHEST)
    tile_width = column_tile.shape[2]
    columns = column_tile.reshape(BPT, NR, tile_width)
    smoothed = jnp.einsum("rq,kqc->rkc", radial_smoother, columns, precision=lax.Precision.HIGHEST)
    shells = lax.all_to_all(smoothed, "sp", split_axis=0, concat_axis=1, tiled=True)
    ev_index = lax.axis_index("ev")
    levels = shell_level.astype(jnp.float32)[:, None, None]
    scale_here = lax.dynamic_slice_in_dim(lateral_scale, ev_index * tile_width, tile_width, 1)
    coefficient = diffusion_rate * levels * scale_here[None]
    kernel_field = shells
    for repeat in range(PASSES):
        padded = padded_2(kernel_field, (("ev", 2),), 1)
        padded = jnp.pad(padded, ((0, 0), (1, 1), (0, 0)))
        beside = (
            padded[:, 2:, 1:-1] + padded[:, :-2, 1:-1] + padded[:, 1:-1, 2:] + padded[:, 1:-1, :-2]
        )
        kernel_field = kernel_field + coefficient * (beside - 4.0 * kernel_field)
    return kernel_field


def solution(mesh):
    placed = (P("ev", None, "sp", None), P("ev", "sp"), P(), P("sp"), P())
    return jax.shard_map(
        per_device, mesh=mesh, in_specs=placed, out_specs=P("sp", None, "ev"), check_vma=False
    )
```

profile of v0, /device:TPU:88, one launch (start us, length us, event | category | flops | bytes accessed | tf_op | source)
XLA Modules:
  0.0 168.2 jit_solution(15304359649547561368)
XLA Ops:
  3.9 7.3 %all-to-all-start = ((f32[1,16,1]{2,0,1:T(1,128)}), f32[1,16,1]{2,0,1:T(1,128)S(1)}, u32[]{:S(2)}, u32[]{:S(2)}) async-start(f32[1,16,1]{2,0,1:T(1,128)} %copy.28), calls=%async_computation | async-start | bytes 16384 | tf_op jit(solution)/shard_map/all_to_all | solution.py:55
  11.1 1.3 convolution_bitcast_fusion.1
  13.2 2.7 %all-to-all-done = f32[1,16,1]{2,0,1:T(1,128)S(1)} async-done(((f32[1,16,1]{2,0,1:T(1,128)}), f32[1,16,1]{2,0,1:T(1,128)S(1)}, u32[]{:S(2)}, u32[]{:S(2)}) %all-to-all-start) | async-done | bytes 96 | tf_op jit(solution)/shard_map/all_to_all | solution.py:55
  15.8 6.3 %all-to-all-start.1 = ((f32[32,16,128]{2,0,1:T(8,128)}), f32[32,16,128]{2,0,1:T(8,128)S(1)}, u32[]{:S(2)}, u32[]{:S(2)}) async-start(f32[32,16,128]{2,0,1:T(8,128)} %copy.29), calls=%async_computation.1 | async-start | bytes 524288 | tf_op jit(solution)/shard_map/all_to_all | solution.py:54
  22.4 5.6 %all-to-all-done.1 = f32[32,16,128]{2,0,1:T(8,128)S(1)} async-done(((f32[32,16,128]{2,0,1:T(8,128)}), f32[32,16,128]{2,0,1:T(8,128)S(1)}, u32[]{:S(2)}, u32[]{:S(2)}) %all-to-all-start.1) | async-done | bytes 262176 | tf_op jit(solution)/shard_map/all_to_all | solution.py:54
  30.9 16.2 %all-to-all-start.2 = ((f32[128,8,128]{2,1,0:T(8,128)}), f32[128,8,128]{2,1,0:T(8,128)S(1)}, u32[]{:S(2)}, u32[]{:S(2)}) async-start(f32[128,8,128]{2,1,0:T(8,128)} %copy.33), calls=%async_computation.2 | async-start | bytes 1048576 | tf_op jit(solution)/shard_map/all_to_all | solution.py:64
  47.1 29.4 %all-to-all-done.2 = f32[128,8,128]{2,1,0:T(8,128)S(1)} async-done(((f32[128,8,128]{2,1,0:T(8,128)}), f32[128,8,128]{2,1,0:T(8,128)S(1)}, u32[]{:S(2)}, u32[]{:S(2)}) %all-to-all-start.2) | async-done | bytes 524320 | tf_op jit(solution)/shard_map/all_to_all | solution.py:64
  76.7 5.4 %collective-permute-start.1 = (f32[2,512,1]{2,1,0:T(8,128)S(1)}, f32[2,512,1]{2,1,0:T(8,128)S(1)}, u32[]{:S(2)}, u32[]{:S(2)}) collective-permute-start(f32[2,512,1]{2,1,0:T(8,128)S(1)} %get-tuple-element.11), channel_id=1, source_target_pairs={{64,0},{128,64},{192,128},{256,192},{320,256},{384,320},{448,384},... | collective-permute-start | bytes 12296 | tf_op jit(solution)/shard_map/ppermute | solution.py:26
  82.1 1.9 %collective-permute-start = (f32[2,512,1]{2,1,0:T(8,128)S(1)}, f32[2,512,1]{2,1,0:T(8,128)S(1)}, u32[]{:S(2)}, u32[]{:S(2)}) collective-permute-start(f32[2,512,1]{2,1,0:T(8,128)S(1)} %get-tuple-element.12), channel_id=1, source_target_pairs={{0,64},{64,128},{128,192},{192,256},{256,320},{320,384},{384,448},... | collective-permute-start | bytes 12296 | tf_op jit(solution)/shard_map/ppermute | solution.py:24
  84.1 10.0 %collective-permute-done.1 = f32[2,512,1]{2,1,0:T(8,128)S(1)} collective-permute-done((f32[2,512,1]{2,1,0:T(8,128)S(1)}, f32[2,512,1]{2,1,0:T(8,128)S(1)}, u32[]{:S(2)}, u32[]{:S(2)}) %collective-permute-start.1) | collective-permute-done | bytes 4128 | tf_op jit(solution)/shard_map/ppermute | solution.py:26
  94.1 7.7 %collective-permute-done = f32[2,512,1]{2,1,0:T(8,128)S(1)} collective-permute-done((f32[2,512,1]{2,1,0:T(8,128)S(1)}, f32[2,512,1]{2,1,0:T(8,128)S(1)}, u32[]{:S(2)}, u32[]{:S(2)}) %collective-permute-start) | collective-permute-done | bytes 4128 | tf_op jit(solution)/shard_map/ppermute | solution.py:24
  103.3 1.9 %collective-permute-start.3 = (f32[2,512,1]{2,1,0:T(8,128)S(1)}, f32[2,512,1]{2,1,0:T(8,128)S(1)}, u32[]{:S(2)}, u32[]{:S(2)}) collective-permute-start(f32[2,512,1]{2,1,0:T(8,128)S(1)} %get-tuple-element.9), channel_id=1, source_target_pairs={{64,0},{128,64},{192,128},{256,192},{320,256},{384,320},{448,384},... | collective-permute-start | bytes 12296 | tf_op jit(solution)/shard_map/ppermute | solution.py:26
  105.3 3.9 %collective-permute-start.2 = (f32[2,512,1]{2,1,0:T(8,128)S(1)}, f32[2,512,1]{2,1,0:T(8,128)S(1)}, u32[]{:S(2)}, u32[]{:S(2)}) collective-permute-start(f32[2,512,1]{2,1,0:T(8,128)S(1)} %get-tuple-element.10), channel_id=1, source_target_pairs={{0,64},{64,128},{128,192},{192,256},{256,320},{320,384},{384,448},... | collective-permute-start | bytes 12296 | tf_op jit(solution)/shard_map/ppermute | solution.py:24
  109.2 9.4 %collective-permute-done.3 = f32[2,512,1]{2,1,0:T(8,128)S(1)} collective-permute-done((f32[2,512,1]{2,1,0:T(8,128)S(1)}, f32[2,512,1]{2,1,0:T(8,128)S(1)}, u32[]{:S(2)}, u32[]{:S(2)}) %collective-permute-start.3) | collective-permute-done | bytes 4128 | tf_op jit(solution)/shard_map/ppermute | solution.py:26
  118.6 5.5 %collective-permute-done.2 = f32[2,512,1]{2,1,0:T(8,128)S(1)} collective-permute-done((f32[2,512,1]{2,1,0:T(8,128)S(1)}, f32[2,512,1]{2,1,0:T(8,128)S(1)}, u32[]{:S(2)}, u32[]{:S(2)}) %collective-permute-start.2) | collective-permute-done | bytes 4128 | tf_op jit(solution)/shard_map/ppermute | solution.py:24
  125.6 1.9 %collective-permute-start.5 = (f32[2,512,1]{2,1,0:T(8,128)S(1)}, f32[2,512,1]{2,1,0:T(8,128)S(1)}, u32[]{:S(2)}, u32[]{:S(2)}) collective-permute-start(f32[2,512,1]{2,1,0:T(8,128)S(1)} %get-tuple-element.7), channel_id=1, source_target_pairs={{64,0},{128,64},{192,128},{256,192},{320,256},{384,320},{448,384},... | collective-permute-start | bytes 12296 | tf_op jit(solution)/shard_map/ppermute | solution.py:26
  127.6 3.9 %collective-permute-start.4 = (f32[2,512,1]{2,1,0:T(8,128)S(1)}, f32[2,512,1]{2,1,0:T(8,128)S(1)}, u32[]{:S(2)}, u32[]{:S(2)}) collective-permute-start(f32[2,512,1]{2,1,0:T(8,128)S(1)} %get-tuple-element.8), channel_id=1, source_target_pairs={{0,64},{64,128},{128,192},{192,256},{256,320},{320,384},{384,448},... | collective-permute-start | bytes 12296 | tf_op jit(solution)/shard_map/ppermute | solution.py:24
  131.5 8.6 %collective-permute-done.5 = f32[2,512,1]{2,1,0:T(8,128)S(1)} collective-permute-done((f32[2,512,1]{2,1,0:T(8,128)S(1)}, f32[2,512,1]{2,1,0:T(8,128)S(1)}, u32[]{:S(2)}, u32[]{:S(2)}) %collective-permute-start.5) | collective-permute-done | bytes 4128 | tf_op jit(solution)/shard_map/ppermute | solution.py:26
  140.0 5.5 %collective-permute-done.4 = f32[2,512,1]{2,1,0:T(8,128)S(1)} collective-permute-done((f32[2,512,1]{2,1,0:T(8,128)S(1)}, f32[2,512,1]{2,1,0:T(8,128)S(1)}, u32[]{:S(2)}, u32[]{:S(2)}) %collective-permute-start.4) | collective-permute-done | bytes 4128 | tf_op jit(solution)/shard_map/ppermute | solution.py:24
  147.1 1.9 %collective-permute-start.7 = (f32[2,512,1]{2,1,0:T(8,128)S(1)}, f32[2,512,1]{2,1,0:T(8,128)S(1)}, u32[]{:S(2)}, u32[]{:S(2)}) collective-permute-start(f32[2,512,1]{2,1,0:T(8,128)S(1)} %get-tuple-element.5), channel_id=1, source_target_pairs={{64,0},{128,64},{192,128},{256,192},{320,256},{384,320},{448,384},... | collective-permute-start | bytes 12296 | tf_op jit(solution)/shard_map/ppermute | solution.py:26
  149.0 3.9 %collective-permute-start.6 = (f32[2,512,1]{2,1,0:T(8,128)S(1)}, f32[2,512,1]{2,1,0:T(8,128)S(1)}, u32[]{:S(2)}, u32[]{:S(2)}) collective-permute-start(f32[2,512,1]{2,1,0:T(8,128)S(1)} %get-tuple-element.6), channel_id=1, source_target_pairs={{0,64},{64,128},{128,192},{192,256},{256,320},{320,384},{384,448},... | collective-permute-start | bytes 12296 | tf_op jit(solution)/shard_map/ppermute | solution.py:24
  152.9 7.7 %collective-permute-done.7 = f32[2,512,1]{2,1,0:T(8,128)S(1)} collective-permute-done((f32[2,512,1]{2,1,0:T(8,128)S(1)}, f32[2,512,1]{2,1,0:T(8,128)S(1)}, u32[]{:S(2)}, u32[]{:S(2)}) %collective-permute-start.7) | collective-permute-done | bytes 4128 | tf_op jit(solution)/shard_map/ppermute | solution.py:26
  160.6 5.5 %collective-permute-done.6 = f32[2,512,1]{2,1,0:T(8,128)S(1)} collective-permute-done((f32[2,512,1]{2,1,0:T(8,128)S(1)}, f32[2,512,1]{2,1,0:T(8,128)S(1)}, u32[]{:S(2)}, u32[]{:S(2)}) %collective-permute-start.6) | collective-permute-done | bytes 4128 | tf_op jit(solution)/shard_map/ppermute | solution.py:24
  166.6 1.5 fusion.6
  (32 shorter events, 12.8 us)
Async XLA Ops:
  0.0 84.1 %copy-start = (f32[512,1024]{1,0:T(8,128)S(1)}, f32[512,1024]{1,0:T(8,128)}, u32[]{:S(2)}) copy-start(f32[512,1024]{1,0:T(8,128)} %param.9) | copy-start | bytes 6291460
  3.9 12.0 %all-to-all-start = ((f32[1,16,1]{2,0,1:T(1,128)}), f32[1,16,1]{2,0,1:T(1,128)S(1)}, u32[]{:S(2)}, u32[]{:S(2)}) async-start(f32[1,16,1]{2,0,1:T(1,128)} %copy.28), calls=%async_computation | async-start | bytes 16384 | tf_op jit(solution)/shard_map/all_to_all | solution.py:55
  13.2 15.7 %copy-start.1 = (f32[128,128]{1,0:T(8,128)S(1)}, f32[128,128]{1,0:T(8,128)}, u32[]{:S(2)}) copy-start(f32[128,128]{1,0:T(8,128)} %param.7) | copy-start | bytes 196612
  15.8 12.1 %all-to-all-start.1 = ((f32[32,16,128]{2,0,1:T(8,128)}), f32[32,16,128]{2,0,1:T(8,128)S(1)}, u32[]{:S(2)}, u32[]{:S(2)}) async-start(f32[32,16,128]{2,0,1:T(8,128)} %copy.29), calls=%async_computation.1 | async-start | bytes 524288 | tf_op jit(solution)/shard_map/all_to_all | solution.py:54
  29.9 17.2 %copy-start.2 = (s32[2]{0:T(128)S(1)}, s32[2]{0:T(128)}, u32[]{:S(2)}) copy-start(s32[2]{0:T(128)} %param.8) | copy-start | bytes 28
  30.9 45.6 %all-to-all-start.2 = ((f32[128,8,128]{2,1,0:T(8,128)}), f32[128,8,128]{2,1,0:T(8,128)S(1)}, u32[]{:S(2)}, u32[]{:S(2)}) async-start(f32[128,8,128]{2,1,0:T(8,128)} %copy.33), calls=%async_computation.2 | async-start | bytes 1048576 | tf_op jit(solution)/shard_map/all_to_all | solution.py:64
  76.7 17.4 %collective-permute-start.1 = (f32[2,512,1]{2,1,0:T(8,128)S(1)}, f32[2,512,1]{2,1,0:T(8,128)S(1)}, u32[]{:S(2)}, u32[]{:S(2)}) collective-permute-start(f32[2,512,1]{2,1,0:T(8,128)S(1)} %get-tuple-element.11), channel_id=1, source_target_pairs={{64,0},{128,64},{192,128},{256,192},{320,256},{384,320},{448,384},... | collective-permute-start | bytes 12296 | tf_op jit(solution)/shard_map/ppermute | solution.py:26
  82.1 19.7 %collective-permute-start = (f32[2,512,1]{2,1,0:T(8,128)S(1)}, f32[2,512,1]{2,1,0:T(8,128)S(1)}, u32[]{:S(2)}, u32[]{:S(2)}) collective-permute-start(f32[2,512,1]{2,1,0:T(8,128)S(1)} %get-tuple-element.12), channel_id=1, source_target_pairs={{0,64},{64,128},{128,192},{192,256},{256,320},{320,384},{384,448},... | collective-permute-start | bytes 12296 | tf_op jit(solution)/shard_map/ppermute | solution.py:24
  103.3 15.3 %collective-permute-start.3 = (f32[2,512,1]{2,1,0:T(8,128)S(1)}, f32[2,512,1]{2,1,0:T(8,128)S(1)}, u32[]{:S(2)}, u32[]{:S(2)}) collective-permute-start(f32[2,512,1]{2,1,0:T(8,128)S(1)} %get-tuple-element.9), channel_id=1, source_target_pairs={{64,0},{128,64},{192,128},{256,192},{320,256},{384,320},{448,384},... | collective-permute-start | bytes 12296 | tf_op jit(solution)/shard_map/ppermute | solution.py:26
  105.3 18.9 %collective-permute-start.2 = (f32[2,512,1]{2,1,0:T(8,128)S(1)}, f32[2,512,1]{2,1,0:T(8,128)S(1)}, u32[]{:S(2)}, u32[]{:S(2)}) collective-permute-start(f32[2,512,1]{2,1,0:T(8,128)S(1)} %get-tuple-element.10), channel_id=1, source_target_pairs={{0,64},{64,128},{128,192},{192,256},{256,320},{320,384},{384,448},... | collective-permute-start | bytes 12296 | tf_op jit(solution)/shard_map/ppermute | solution.py:24
  125.6 14.4 %collective-permute-start.5 = (f32[2,512,1]{2,1,0:T(8,128)S(1)}, f32[2,512,1]{2,1,0:T(8,128)S(1)}, u32[]{:S(2)}, u32[]{:S(2)}) collective-permute-start(f32[2,512,1]{2,1,0:T(8,128)S(1)} %get-tuple-element.7), channel_id=1, source_target_pairs={{64,0},{128,64},{192,128},{256,192},{320,256},{384,320},{448,384},... | collective-permute-start | bytes 12296 | tf_op jit(solution)/shard_map/ppermute | solution.py:26
  127.6 18.0 %collective-permute-start.4 = (f32[2,512,1]{2,1,0:T(8,128)S(1)}, f32[2,512,1]{2,1,0:T(8,128)S(1)}, u32[]{:S(2)}, u32[]{:S(2)}) collective-permute-start(f32[2,512,1]{2,1,0:T(8,128)S(1)} %get-tuple-element.8), channel_id=1, source_target_pairs={{0,64},{64,128},{128,192},{192,256},{256,320},{320,384},{384,448},... | collective-permute-start | bytes 12296 | tf_op jit(solution)/shard_map/ppermute | solution.py:24
  147.1 13.6 %collective-permute-start.7 = (f32[2,512,1]{2,1,0:T(8,128)S(1)}, f32[2,512,1]{2,1,0:T(8,128)S(1)}, u32[]{:S(2)}, u32[]{:S(2)}) collective-permute-start(f32[2,512,1]{2,1,0:T(8,128)S(1)} %get-tuple-element.5), channel_id=1, source_target_pairs={{64,0},{128,64},{192,128},{256,192},{320,256},{384,320},{448,384},... | collective-permute-start | bytes 12296 | tf_op jit(solution)/shard_map/ppermute | solution.py:26
  149.0 17.2 %collective-permute-start.6 = (f32[2,512,1]{2,1,0:T(8,128)S(1)}, f32[2,512,1]{2,1,0:T(8,128)S(1)}, u32[]{:S(2)}, u32[]{:S(2)}) collective-permute-start(f32[2,512,1]{2,1,0:T(8,128)S(1)} %get-tuple-element.6), channel_id=1, source_target_pairs={{0,64},{64,128},{128,192},{192,256},{256,320},{320,384},{384,448},... | collective-permute-start | bytes 12296 | tf_op jit(solution)/shard_map/ppermute | solution.py:24
where the time goes:
time: 169 us; the launch traced here: 168 us
  waiting for transfers between devices  97.7 us (58%)
  starting transfers between devices  54.6 us (32%)
  other arithmetic  8.32 us (5%)
  local copies, waits for them, and re-layouts  3.67 us (2%)
  matrix products  3.66 us (2%)
    ppermute x4, waiting for transfers between devices, padded_2(): lax.ppermute(head, axis, [((i + 1) % count, i) for i in range(ends)])  35.7 us
    all_to_all x1, waiting for transfers between devices, per_device(): lax.all_to_all(smoothed, 'sp', split_axis=0, concat_axis=1, tiled=True)  29.4 us
    ppermute x4, waiting for transfers between devices, padded_2(): lax.ppermute(tail, axis, [(i, (i + 1) % count) for i in range(ends)])  24.4 us
    all_to_all x1, starting transfers between devices, per_device(): lax.all_to_all(smoothed, 'sp', split_axis=0, concat_axis=1, tiled=True)  16.2 us
    ppermute x4, starting transfers between devices, padded_2(): lax.ppermute(tail, axis, [(i, (i + 1) % count) for i in range(ends)])  13.7 us
    ppermute x4, starting transfers between devices, padded_2(): lax.ppermute(head, axis, [((i + 1) % count, i) for i in range(ends)])  11.2 us
    all_to_all x1, starting transfers between devices, per_device(): lax.all_to_all(label_out, 'ev', split_axis=1, concat_axis=1, tiled=True)  7.26 us
    all_to_all x1, starting transfers between devices, per_device(): lax.all_to_all(packed, 'ev', split_axis=1, concat_axis=1, tiled=True)  6.3 us
  transfers between devices with their start and end apart: 11, of which 11 were waited for; matrix products, arithmetic and copies ran while one was open for 1% of the time, Pallas kernels for 0%

commit v1 on v0

v1 whole, which is shorter than its diff:
```python
import functools

import jax
import jax.numpy as jnp
from jax import lax
from jax.experimental import pallas as pl
from jax.experimental.pallas import tpu as pltpu
from jax.sharding import PartitionSpec as P

NR = 128
RB = 32
BY = 128
BPT = 8
CAP = 2
PASSES = 4
NSEG = 4
PER_OWNER = BPT * NSEG
LANES = 128
TILE = 8
MESSAGE = CAP * RB + TILE
LABELS = 64
PIECE = 2 * BPT + 1

diffusion_rate = 0.0615

VMEM = pl.BlockSpec(memory_space=pltpu.VMEM)
SMEM = pl.BlockSpec(memory_space=pltpu.SMEM)
ANY = pl.BlockSpec(memory_space=pl.ANY)


def lane_index(shape=(TILE, LANES)):
    return lax.broadcasted_iota(jnp.int32, shape, len(shape) - 1)


def pack_kernel(owners, ids_ref, blocks_ref, out_ref):
    listed = ids_ref.shape[1]
    lane = lane_index()
    zero = jnp.zeros((TILE, LANES), jnp.float32)
    for row in range(0, owners * MESSAGE, TILE):
        out_ref[row : row + TILE, :] = zero
    ids = [ids_ref[0, j] for j in range(listed)]
    owner_of = [lax.shift_right_logical(i, 5) for i in ids]
    for j in range(listed):
        owner = owner_of[j]
        within = lax.bitwise_and(ids[j], PER_OWNER - 1).astype(jnp.float32)
        rank = jnp.int32(0)
        for i in range(j):
            rank = rank + jnp.where(owner_of[i] == owner, 1, 0)
        base = owner * MESSAGE
        first = zero
        last = zero
        for a in range(RB // TILE):
            cells = blocks_ref[pl.ds(a * TILE * listed + j, TILE, stride=listed), :]
            start = pl.multiple_of(base + rank * RB + a * TILE, TILE)
            out_ref[pl.ds(start, TILE), :] = cells
            head = jnp.where(lane < 4, cells, 0.0)
            tail = jnp.where(lane >= LANES - 4, cells, 0.0)
            first = first + (pltpu.roll(head, 16 * a, 1) if a else head)
            last = last + pltpu.roll(tail, 16 * a + 4, 1)
        edge = pl.multiple_of(base + CAP * RB, TILE)
        here = pl.ds(edge, TILE)
        out_ref[here, :] = out_ref[here, :] + jnp.where(lane == LABELS + rank, within, 0.0)
        later = rank == 1
        to_left = jnp.where(later, pltpu.roll(first, 12, 1), pltpu.roll(first, 8, 1))
        to_left = to_left + jnp.where(lane == LABELS + 4 + rank, within, 0.0)
        to_right = jnp.where(later, pltpu.roll(last, 4, 1), last)
        to_right = to_right + jnp.where(lane == LABELS + 2 + rank, within, 0.0)

        @pl.when(owner > 0)
        def _():
            there = pl.ds(pl.multiple_of(edge - MESSAGE, TILE), TILE)
            out_ref[there, :] = out_ref[there, :] + to_left

        @pl.when(owner < owners - 1)
        def _():
            there = pl.ds(pl.multiple_of(edge + MESSAGE, TILE), TILE)
            out_ref[there, :] = out_ref[there, :] + to_right


def smooth_kernel(groups, arrived_hbm, smoother_ref, out_ref, arrived_ref, labels_ref, columns_ref, sems):
    labels_copy = pltpu.make_async_copy(
        arrived_hbm.at[:, pl.ds(CAP * RB, 1), :], labels_ref, sems.at[0]
    )
    cells_copy = pltpu.make_async_copy(arrived_hbm, arrived_ref, sems.at[1])
    labels_copy.start()
    cells_copy.start()
    lane = lane_index()
    columns_ref[...] = jnp.zeros_like(columns_ref)
    labels_copy.wait()
    cells_copy.wait()
    for g in range(groups):
        for rank in range(CAP):
            label = labels_ref[g, 0, LABELS + rank].astype(jnp.int32)
            row = lax.shift_right_logical(label, 2)
            segment = lax.bitwise_and(label, NSEG - 1)
            where = (
                pl.ds(pl.multiple_of(segment * RB, RB), RB),
                pl.ds(pl.multiple_of(row * LANES, LANES), LANES),
            )
            columns_ref[where] = columns_ref[where] + arrived_ref[g, rank * RB : (rank + 1) * RB, :]
        edges = arrived_ref[g, CAP * RB :, :]
        for h in range(2 * CAP):
            label = labels_ref[g, 0, LABELS + 2 + h].astype(jnp.int32)
            row = lax.shift_right_logical(label, 2)
            segment = lax.bitwise_and(label, NSEG - 1)
            target = (BPT - 1 - row) * 8 + (4 if h >= CAP else 0) + LANES
            for a in range(RB // TILE):
                source = 16 * a + 4 * h
                four = jnp.where((lane >= source) & (lane < source + 4), edges, 0.0)
                moved = pltpu.roll(four, lax.bitwise_and(target - source, LANES - 1), 1)
                where = (
                    pl.ds(pl.multiple_of(segment * RB + a * TILE, TILE), TILE),
                    pl.ds(BPT * LANES, LANES),
                )
                columns_ref[where] = columns_ref[where] + moved
    edge_columns = columns_ref[:, BPT * LANES :]
    columns_ref[:, BPT * LANES :] = edge_columns + pltpu.roll(edge_columns, LANES // 2, 1)
    half = NR // 2
    smoother = jnp.concatenate(
        [smoother_ref[pl.ds(0, half, stride=2), :], smoother_ref[pl.ds(1, half, stride=2), :]], axis=0
    )
    for row in range(BPT):
        done = jnp.dot(
            smoother,
            columns_ref[:, row * LANES : (row + 1) * LANES],
            precision=lax.Precision.HIGHEST,
            preferred_element_type=jnp.float32,
        )
        out_ref[pl.ds(row, half, stride=PIECE), :] = done[:half]
        out_ref[pl.ds(BPT + row, half, stride=PIECE), :] = done[half:]
    done = jnp.dot(
        smoother,
        columns_ref[:, BPT * LANES :],
        precision=lax.Precision.HIGHEST,
        preferred_element_type=jnp.float32,
    )
    low = lane_index((half, LANES)) < LANES // 2
    out_ref[pl.ds(2 * BPT, half, stride=PIECE), :] = jnp.where(low, done[:half], done[half:])


def diffuse_kernel(
    owners, cells_ref, level_ref, scale_hbm, out_ref, scale_ref, main_a, main_b, side_a, side_b, sems
):
    shells, rows, width = out_ref.shape
    here = lax.axis_index("ev")
    places = (jnp.maximum(here - 1, 0), here, jnp.minimum(here + 1, owners - 1))
    copies = [
        pltpu.make_async_copy(
            scale_hbm.at[:, pl.ds(pl.multiple_of(place * width, width), width)],
            scale_ref.at[n],
            sems.at[n],
        )
        for n, place in enumerate(places)
    ]
    for copy in copies:
        copy.start()
    lane = lane_index()
    nothing = jnp.zeros((TILE, LANES), jnp.float32)
    for buffer in (main_a, main_b, side_a, side_b):
        for shell in range(shells):
            buffer[shell, 0:TILE, :] = nothing
            buffer[shell, TILE + rows : 2 * TILE + rows, :] = nothing
    is_side = (lane < 4) | (lane >= LANES - 4)
    for stripe in range(rows // BPT):
        at = stripe * PIECE
        wide = jnp.broadcast_to(cells_ref[at + 2 * BPT : at + PIECE, :], (TILE, LANES))
        for shell in range(shells):
            spot = TILE + stripe * BPT
            main_a[shell, spot : spot + BPT, :] = cells_ref[at + shell * BPT : at + (shell + 1) * BPT, :]
            turned = pltpu.roll(wide, 68 - 64 * shell, 1, stride=8, stride_axis=0)
            side_a[shell, spot : spot + BPT, :] = jnp.where(is_side, turned, 0.0)
    for copy in copies:
        copy.wait()
    factors = [diffusion_rate * level_ref[shell].astype(jnp.float32) for shell in range(shells)]
    step = 16
    lane = lane_index((step, LANES))
    is_first = lane == 0
    is_last = lane == LANES - 1
    keep_right = (lane < 4) & (here < owners - 1)
    keep_left = (lane >= LANES - 4) & (here > 0)

    def around(buffer, shell, start):
        above = buffer[shell, start - 1 : start - 1 + step, :]
        middle = buffer[shell, start : start + step, :]
        below = buffer[shell, start + 1 : start + 1 + step, :]
        return above + below, middle, pltpu.roll(middle, 1, 1), pltpu.roll(middle, LANES - 1, 1)

    buffers = ((main_a, side_a), (main_b, side_b))
    for repeat in range(PASSES):
        (main, side), (main_next, side_next) = buffers[repeat % 2], buffers[(repeat + 1) % 2]
        final = repeat == PASSES - 1
        for block in range(rows // step):
            start = TILE + block * step
            at = slice(block * step, (block + 1) * step)
            scale = scale_ref[1, at, :]
            if not final:
                scale_side = jnp.where(
                    keep_right, scale_ref[2, at, :], jnp.where(keep_left, scale_ref[0, at, :], 0.0)
                )
            for shell in range(shells):
                vertical, middle, left, right = around(main, shell, start)
                side_vertical, side_middle, side_left, side_right = around(side, shell, start)
                beside = vertical + jnp.where(is_first, side_left, left) + jnp.where(is_last, side_right, right)
                new = middle + (factors[shell] * scale) * (beside - 4.0 * middle)
                if final:
                    out_ref[shell, at, :] = new
                    continue
                main_next[shell, start : start + step, :] = new
                beside = (
                    side_vertical
                    + jnp.where(is_first, left, side_left)
                    + jnp.where(is_last, right, side_right)
                )
                new = side_middle + (factors[shell] * scale_side) * (beside - 4.0 * side_middle)
                side_next[shell, start : start + step, :] = new


def per_device(partial_kernels, block_ids, radial_smoother, shell_level, lateral_scale):
    owners = lax.axis_size("ev")
    holders = lax.axis_size("sp")
    listed = block_ids.shape[1]
    rows = lateral_scale.shape[0]
    packed = pl.pallas_call(
        functools.partial(pack_kernel, owners),
        out_shape=jax.ShapeDtypeStruct((owners * MESSAGE, LANES), jnp.float32),
        in_specs=[SMEM, VMEM],
        out_specs=VMEM,
    )(block_ids, partial_kernels.reshape(RB * listed, BY))
    arrived = lax.all_to_all(
        packed.reshape(owners, MESSAGE, LANES), "ev", split_axis=0, concat_axis=0, tiled=True
    )
    pieces = pl.pallas_call(
        functools.partial(smooth_kernel, owners),
        out_shape=jax.ShapeDtypeStruct((holders * PIECE, LANES), jnp.float32),
        in_specs=[ANY, VMEM],
        out_specs=VMEM,
        scratch_shapes=[
            pltpu.VMEM((owners, MESSAGE, LANES), jnp.float32),
            pltpu.SMEM((owners, 1, LANES), jnp.float32),
            pltpu.VMEM((NR, (BPT + 1) * LANES), jnp.float32),
            pltpu.SemaphoreType.DMA((2,)),
        ],
    )(arrived, radial_smoother)
    shells = lax.all_to_all(
        pieces.reshape(holders, 1, PIECE * LANES), "sp", split_axis=0, concat_axis=0, tiled=True
    ).reshape(holders * PIECE, LANES)
    mine = shell_level.shape[0]
    field = pltpu.VMEM((mine, rows + 2 * TILE, LANES), jnp.float32)
    return pl.pallas_call(
        functools.partial(diffuse_kernel, owners),
        out_shape=jax.ShapeDtypeStruct((mine, rows, LANES), jnp.float32),
        in_specs=[VMEM, SMEM, ANY],
        out_specs=VMEM,
        scratch_shapes=[
            pltpu.VMEM((3, rows, LANES), jnp.float32),
            field,
            field,
            field,
            field,
            pltpu.SemaphoreType.DMA((3,)),
        ],
    )(shells, shell_level, lateral_scale)


def solution(mesh):
    placed = (P("ev", None, "sp", None), P("ev", "sp"), P(), P("sp"), P())
    return jax.shard_map(
        per_device, mesh=mesh, in_specs=placed, out_specs=P("sp", None, "ev"), check_vma=False
    )
```

time: 169 us -> 79.9 us (0.47)
  the two profiles are of different devices: /device:TPU:88 before, /device:TPU:8 now
where the time goes in v1:
time: 79.9 us; the launch traced here: 79.5 us
  blocking collectives  67.7 us (85%)
  Pallas kernels  11.8 us (15%)
    all_to_all x1, blocking collectives, per_device(): lax.all_to_all(pieces.reshape(holders, 1, PIECE * LANES), 'sp', split_axi...  52.2 us
    all_to_all x1, blocking collectives, per_device(): lax.all_to_all(packed.reshape(owners, MESSAGE, LANES), 'ev', split_axis=0...  15.5 us
    pallas_call x1, Pallas kernels, per_device(): pl.pallas_call(functools.partial(diffuse_kernel, owners), out_shape=jax.S...  5.3 us
    pallas_call x1, Pallas kernels, per_device(): pl.pallas_call(functools.partial(smooth_kernel, owners), out_shape=jax.Sh...  3.71 us
    pallas_call x1, Pallas kernels, per_device(): pl.pallas_call(functools.partial(pack_kernel, owners), out_shape=jax.Shap...  2.81 us

profile of v1, /device:TPU:8, one launch (start us, length us, event | category | flops | bytes accessed | tf_op | source)
XLA Modules:
  0.0 79.5 jit_solution(1177362491811034390)
XLA Ops:
  0.0 2.8 %shard_map.55 = f32[576,128]{1,0:T(8,128)} custom-call(s32[1,8]{1,0:T(1,128)} %ids_ref.1, f32[256,128]{1,0:T(8,128)} %bitcast.7), custom_call_target="tpu_custom_call" | custom-call | tf_op jit(solution)/shard_map/pallas_call | solution.py:223
  2.8 15.5 %all_to_all.10.arrived_hbm = f32[8,72,128]{2,1,0:T(8,128)} all-to-all(f32[8,72,128]{2,1,0:T(8,128)} %bitcast.6), channel_id=1, replica_groups=mesh['ev'=8,'sp'=64] {'ev'}, dimensions={0} | all-to-all | bytes 589824 | tf_op jit(solution)/shard_map/all_to_all | solution.py:229
  18.3 3.7 %shard_map.56 = f32[1088,128]{1,0:T(8,128)} custom-call(f32[8,72,128]{2,1,0:T(8,128)} %all_to_all.10.arrived_hbm, f32[128,128]{1,0:T(8,128)} %smoother_ref.1), custom_call_target="tpu_custom_call" | custom-call | tf_op jit(solution)/shard_map/pallas_call | solution.py:232
  22.0 52.2 %all_to_all.11 = f32[64,1,2176]{2,1,0:T(1,128)} all-to-all(f32[64,1,2176]{2,1,0:T(1,128)} %bitcast.4), channel_id=1, replica_groups=mesh['ev'=8,'sp'=64] {'sp'}, dimensions={0} | all-to-all | bytes 1114112 | tf_op jit(solution)/shard_map/all_to_all | solution.py:244
  74.2 5.3 %shard_map.57 = f32[2,512,128]{2,1,0:T(8,128)} custom-call(f32[1088,128]{1,0:T(8,128)} %bitcast.5, s32[2]{0:T(128)} %level_ref.1, f32[512,1024]{1,0:T(8,128)} %scale_hbm.1), custom_call_target="tpu_custom_call" | custom-call | tf_op jit(solution)/shard_map/pallas_call | solution.py:249

commit v2 on v1

v2 whole, which is shorter than its diff:
```python
import functools

import jax
import jax.numpy as jnp
from jax import lax
from jax.experimental import pallas as pl
from jax.experimental.pallas import tpu as pltpu
from jax.sharding import PartitionSpec as P

NR = 128
RB = 32
BY = 128
BPT = 8
CAP = 2
PASSES = 4
NSEG = 4
PER_OWNER = BPT * NSEG
LANES = 128
TILE = 8
MESSAGE = CAP * RB + TILE
LABELS = 64
STRIP = 16
SIDES = 4
PIECE = 2 * BPT + 1

diffusion_rate = 0.0615

SMALL = pltpu.CompilerParams(vmem_limit_bytes=12 * 1024 * 1024)
VMEM = pl.BlockSpec(memory_space=pltpu.VMEM)
HBM = pl.BlockSpec(memory_space=pltpu.HBM)


def lane_index(shape=(TILE, LANES)):
    return lax.broadcasted_iota(jnp.int32, shape, len(shape) - 1)


def pack_kernel(owners, ids_hbm, blocks_hbm, out_ref, ids_ref, blocks_ref, sems):
    ids_copy = pltpu.make_async_copy(ids_hbm, ids_ref, sems.at[0])
    blocks_copy = pltpu.make_async_copy(blocks_hbm, blocks_ref, sems.at[1])
    ids_copy.start()
    blocks_copy.start()
    listed = ids_ref.shape[1]
    lane = lane_index()
    zero = jnp.zeros((TILE, LANES), jnp.float32)
    for row in range(0, owners * MESSAGE, TILE):
        out_ref[row : row + TILE, :] = zero
    ids_copy.wait()
    ids = [ids_ref[0, j] for j in range(listed)]
    owner_of = [lax.shift_right_logical(i, 5) for i in ids]
    ranks = []
    for j in range(listed):
        rank = jnp.int32(0)
        for i in range(j):
            rank = rank + jnp.where(owner_of[i] == owner_of[j], 1, 0)
        ranks.append(rank)
    blocks_copy.wait()

    def add(owner, cells):
        there = pl.ds(pl.multiple_of(owner * MESSAGE + CAP * RB, TILE), TILE)
        out_ref[there, :] = out_ref[there, :] + cells

    for j in range(listed):
        owner, rank = owner_of[j], ranks[j]
        within = lax.bitwise_and(ids[j], PER_OWNER - 1).astype(jnp.float32)
        first = zero
        last = zero
        for a in range(RB // TILE):
            cells = blocks_ref[pl.ds(a * TILE * listed + j, TILE, stride=listed), :]
            start = pl.multiple_of(owner * MESSAGE + rank * RB + a * TILE, TILE)
            out_ref[pl.ds(start, TILE), :] = cells
            head = jnp.where(lane < 4, cells, 0.0)
            tail = jnp.where(lane >= LANES - 4, cells, 0.0)
            first = first + (pltpu.roll(head, 16 * a, 1) if a else head)
            last = last + pltpu.roll(tail, 16 * a + 4, 1)
        add(owner, jnp.where(lane == LABELS + rank, within, 0.0))
        later = rank == 1
        to_left = jnp.where(later, pltpu.roll(first, 12, 1), pltpu.roll(first, 8, 1))
        to_left = to_left + jnp.where(lane == LABELS + 4 + rank, within, 0.0)
        to_right = jnp.where(later, pltpu.roll(last, 4, 1), last)
        to_right = to_right + jnp.where(lane == LABELS + 2 + rank, within, 0.0)
        add(jnp.maximum(owner - 1, 0), jnp.where(owner > 0, to_left, 0.0))
        add(jnp.minimum(owner + 1, owners - 1), jnp.where(owner < owners - 1, to_right, 0.0))


def halves(cells):
    high = cells.astype(jnp.bfloat16)
    low = (cells - high.astype(jnp.float32)).astype(jnp.bfloat16)
    return high, low


def smooth_kernel(
    groups, arrived_ref, smoother_hbm, out_ref, spots_ref, labels_ref, columns_ref, smoother_ref, sems
):
    smoother_copy = pltpu.make_async_copy(smoother_hbm, smoother_ref, sems.at[1])
    smoother_copy.start()
    labels = arrived_ref[:, CAP * RB, :].astype(jnp.int32)
    rows = lax.shift_right_logical(labels, 2)
    label_lane = lane_index((groups, LANES)) - (LABELS + CAP)
    shift = jnp.where(label_lane >= CAP, 4, 0)
    spots_ref[0] = lax.bitwise_and(labels, NSEG - 1) * RB
    spots_ref[1] = rows * LANES
    spots_ref[2] = (BPT - 1 - rows) * 8 + shift
    labels_copy = pltpu.make_async_copy(spots_ref, labels_ref, sems.at[0])
    labels_copy.start()
    lane = lane_index()
    lane_four = lax.bitwise_and(lane, ~3)
    columns_ref[...] = jnp.zeros_like(columns_ref)
    labels_copy.wait()
    for g in range(groups):
        for rank in range(CAP):
            where = (
                pl.ds(pl.multiple_of(labels_ref[0, g, LABELS + rank], RB), RB),
                pl.ds(pl.multiple_of(labels_ref[1, g, LABELS + rank], LANES), LANES),
            )
            columns_ref[where] = columns_ref[where] + arrived_ref[g, rank * RB : (rank + 1) * RB, :]
    for g in range(groups):
        edges = arrived_ref[g, CAP * RB :, :]
        for h in range(2 * CAP):
            target = labels_ref[2, g, LABELS + CAP + h]
            keep = lane_four == target
            turned = pltpu.roll(edges, lax.bitwise_and(target + (LANES - 4 * h), LANES - 1), 1)
            parts = [turned] + [
                pltpu.roll(turned, LANES - 16 * a, 1) for a in range(1, RB // TILE)
            ]
            four = jnp.concatenate([jnp.where(keep, part, 0.0) for part in parts], axis=0)
            where = (
                pl.ds(pl.multiple_of(labels_ref[0, g, LABELS + CAP + h], RB), RB),
                pl.ds(BPT * LANES, LANES),
            )
            columns_ref[where] = columns_ref[where] + four
    edge_columns = columns_ref[:, BPT * LANES :]
    columns_ref[:, BPT * LANES :] = edge_columns + pltpu.roll(edge_columns, LANES // 2, 1)
    smoother_copy.wait()
    half = NR // 2
    smoother = jnp.concatenate(
        [smoother_ref[pl.ds(0, half, stride=2), :], smoother_ref[pl.ds(1, half, stride=2), :]], axis=0
    )
    high, low = halves(smoother)
    twice = jnp.concatenate([high, high], axis=1)

    def smoothed(start, width):
        first, second = halves(columns_ref[:, start : start + width])
        both = jnp.concatenate([first, second], axis=0)
        return jnp.dot(twice, both, preferred_element_type=jnp.float32) + jnp.dot(
            low, first, preferred_element_type=jnp.float32
        )

    for row in range(0, BPT, 2):
        done = smoothed(row * LANES, 2 * LANES)
        for i in range(2):
            cells = done[:, i * LANES : (i + 1) * LANES]
            out_ref[pl.ds(row + i, half, stride=PIECE), :] = cells[:half]
            out_ref[pl.ds(BPT + row + i, half, stride=PIECE), :] = cells[half:]
    done = smoothed(BPT * LANES, LANES)
    lower = lane_index((half, LANES)) < LANES // 2
    out_ref[pl.ds(2 * BPT, half, stride=PIECE), :] = jnp.where(lower, done[:half], done[half:])


def diffuse_kernel(
    owners, cells_ref, level_hbm, scale_ref, out_hbm,
    level_ref, main_a, main_b, side_a, side_b, side_scale, centre_ref, beside_ref, out_ref,
    near_ref, side_near_ref, edge_ref, sems,
):
    shells, rows, width = out_ref.shape
    level_copy = pltpu.make_async_copy(level_hbm, level_ref, sems.at[SIDES])
    level_copy.start()
    here = lax.axis_index("ev")
    own = pl.multiple_of(here * width, width)
    before = pl.multiple_of(jnp.maximum(here - 1, 0) * width, width)
    after = pl.multiple_of(jnp.minimum(here + 1, owners - 1) * width, width)
    nothing = jnp.zeros((TILE, LANES), jnp.float32)
    stripes = rows // BPT
    tiles = stripes // SIDES
    side_rows = tiles * TILE
    chunk = 8 * TILE
    for buffer in (main_a, main_b):
        for shell in range(shells):
            buffer[shell, 0:TILE, :] = nothing
            buffer[shell, TILE + rows : 2 * TILE + rows, :] = nothing

    row_of = lax.broadcasted_iota(jnp.int32, (LANES, LANES), 0)
    lane_of = lax.broadcasted_iota(jnp.int32, (LANES, LANES), 1)

    def ones(chosen):
        return jnp.where(chosen, 1.0, 0.0).astype(jnp.bfloat16)

    near = ones(jnp.abs(row_of - lane_of) == 1)
    near_ref[0:LANES, :] = near
    near_ref[LANES:, :] = near
    from_in, to_in = lax.bitwise_and(row_of, STRIP - 1), lax.bitwise_and(lane_of, STRIP - 1)
    same_strip = lax.shift_right_logical(row_of, 4) == lax.shift_right_logical(lane_of, 4)
    same_run = lax.shift_right_logical(row_of, 2) == lax.shift_right_logical(lane_of, 2)
    joined = (jnp.abs(from_in - to_in) == 7) & (jnp.maximum(from_in, to_in) == 11)
    joined = joined | ((jnp.abs(from_in - to_in) == 9) & (jnp.maximum(from_in, to_in) == 12))
    side_near = ones(((jnp.abs(row_of - lane_of) == 1) & same_run) | (joined & same_strip))
    exchanged = jnp.where(to_in == 11, lane_of + 1, jnp.where(to_in == 12, lane_of - 1, lane_of))
    exchange = ones(row_of == exchanged)
    for part in range(2):
        at = slice(part * LANES, (part + 1) * LANES)
        side_near_ref[at, 0:LANES] = side_near
        side_near_ref[at, LANES:] = exchange

    lane = lane_index()
    spot_in = lax.bitwise_and(lane, STRIP - 1)
    in_strip = [(lane >= STRIP * n) & (lane < STRIP * (n + 1)) for n in range(2 * SIDES)]
    inner = spot_in < 8
    outer = spot_in >= 8
    for v in range(tiles):
        side = nothing
        for n in range(SIDES):
            stripe = n * tiles + v
            at = stripe * PIECE
            spot = TILE + stripe * BPT
            wide = jnp.broadcast_to(cells_ref[at + 2 * BPT : at + PIECE, :], (TILE, LANES))
            turned = pltpu.roll(wide, STRIP * (n + 1), 1, stride=8, stride_axis=0)
            side = jnp.where((in_strip[n] | in_strip[SIDES + n]) & outer, turned, side)
            for shell in range(shells):
                cells = cells_ref[at + shell * BPT : at + (shell + 1) * BPT, :]
                main_a[shell, spot : spot + BPT, :] = cells
                slot = (1 - shell) * SIDES + n
                side = jnp.where(
                    in_strip[slot] & inner, pltpu.roll(cells, STRIP * slot + 4, 1), side
                )
        side_a[TILE + v * TILE : 2 * TILE + v * TILE, :] = side
    keep_after = (lane < 4) & (here < owners - 1)
    keep_before = (lane >= LANES - 4) & (here > 0)
    for v in range(tiles):
        scale = nothing
        for n in range(SIDES):
            stripe = n * tiles + v
            at = slice(stripe * BPT, (stripe + 1) * BPT)
            beyond = jnp.where(
                keep_after,
                scale_ref[at, pl.ds(after, width)],
                jnp.where(keep_before, scale_ref[at, pl.ds(before, width)], 0.0),
            )
            mine = pltpu.roll(scale_ref[at, pl.ds(own, width)], STRIP * n + 4, 1)
            scale = jnp.where(in_strip[n] & inner, mine, scale)
            scale = jnp.where(in_strip[n] & outer, pltpu.roll(beyond, STRIP * n + 12, 1), scale)
        side_scale[v * TILE : (v + 1) * TILE, :] = scale + pltpu.roll(scale, LANES // 2, 1)

    lane_row = lane_index((1, LANES))
    stripe_in = lax.bitwise_and(lane_row, SIDES * STRIP - 1)
    last_row = TILE + side_rows - 1

    def join(side):
        down = pltpu.roll(side[last_row : last_row + 1, :], STRIP, 1)
        side[TILE - 1 : TILE, :] = jnp.where(stripe_in < STRIP, 0.0, down)
        up = pltpu.roll(side[TILE : TILE + 1, :], LANES - STRIP, 1)
        side[last_row + 1 : last_row + 2, :] = jnp.where(stripe_in >= (SIDES - 1) * STRIP, 0.0, up)

    join(side_a)
    level_copy.wait()
    factors = [diffusion_rate * level_ref[shell].astype(jnp.float32) for shell in range(shells)]
    chunk_lane = lane_index((chunk, LANES))
    is_edge = (chunk_lane == 0) | (chunk_lane == LANES - 1)
    side_factor = jnp.where(chunk_lane < LANES // 2, factors[1], factors[0])
    copies = []
    buffers = ((main_a, side_a), (main_b, side_b))
    for repeat in range(PASSES):
        (main, side), (main_next, side_next) = buffers[repeat % 2], buffers[(repeat + 1) % 2]
        final = repeat == PASSES - 1
        for start in range(0, side_rows, chunk):
            at = slice(TILE + start, TILE + start + chunk)
            middle = side[at, :]
            sums = jnp.dot(
                jnp.concatenate(halves(middle), axis=1),
                side_near_ref[...],
                preferred_element_type=jnp.float32,
            )
            edge_ref[start : start + chunk, :] = sums[:, LANES:]
            if not final:
                vertical = side[at.start - 1 : at.stop - 1, :] + side[at.start + 1 : at.stop + 1, :]
                coefficient = side_factor * side_scale[start : start + chunk, :]
                side_next[at, :] = middle + coefficient * (
                    (vertical + sums[:, :LANES]) - 4.0 * middle
                )
        if not final:
            join(side_next)
        for n in range(SIDES):
            for shell in range(shells):
                slot = (1 - shell) * SIDES + n
                for part in range(0, side_rows, chunk):
                    edge = edge_ref[part : part + chunk, :]
                    start = n * side_rows + part
                    at = slice(start, start + chunk)
                    first = TILE + start
                    middle = main[shell, first : first + chunk, :]
                    sums = jnp.dot(
                        jnp.concatenate(halves(middle), axis=1),
                        near_ref[...],
                        preferred_element_type=jnp.float32,
                    )
                    turned = pltpu.roll(edge, (2 * LANES - STRIP * slot - 12) % LANES, 1)
                    vertical = (
                        main[shell, first - 1 : first + chunk - 1, :]
                        + main[shell, first + 1 : first + chunk + 1, :]
                    )
                    if repeat == 0:
                        coefficient = factors[shell] * scale_ref[at, pl.ds(own, width)]
                        centre = 1.0 - 4.0 * coefficient
                        beside_ref[shell, at, :] = coefficient
                        centre_ref[shell, at, :] = centre
                    else:
                        coefficient = beside_ref[shell, at, :]
                        centre = centre_ref[shell, at, :]
                    sums = (vertical + sums) + jnp.where(is_edge, turned, 0.0)
                    new = centre * middle + coefficient * sums
                    if final:
                        out_ref[shell, at, :] = new
                    else:
                        main_next[shell, first : first + chunk, :] = new
            if final:
                done = pl.ds(n * side_rows, side_rows)
                copy = pltpu.make_async_copy(out_ref.at[:, done, :], out_hbm.at[:, done, :], sems.at[n])
                copy.start()
                copies.append(copy)
    for copy in copies:
        copy.wait()


def in_hbm(array):
    return pltpu.with_memory_space_constraint(array, pltpu.HBM)


def per_device(partial_kernels, block_ids, radial_smoother, shell_level, lateral_scale):
    owners = lax.axis_size("ev")
    holders = lax.axis_size("sp")
    listed = block_ids.shape[1]
    rows, columns = lateral_scale.shape
    mine = shell_level.shape[0]
    packed = pl.pallas_call(
        functools.partial(pack_kernel, owners),
        out_shape=jax.ShapeDtypeStruct((owners * MESSAGE, LANES), jnp.float32),
        in_specs=[HBM, HBM],
        out_specs=VMEM,
        scratch_shapes=[
            pltpu.SMEM((1, listed), jnp.int32),
            pltpu.VMEM((RB * listed, LANES), jnp.float32),
            pltpu.SemaphoreType.DMA((2,)),
        ],
        compiler_params=SMALL,
    )(in_hbm(block_ids), in_hbm(partial_kernels.reshape(RB * listed, BY)))
    arrived = lax.all_to_all(
        packed.reshape(owners, MESSAGE, LANES), "ev", split_axis=0, concat_axis=0, tiled=True
    )
    pieces = pl.pallas_call(
        functools.partial(smooth_kernel, owners),
        out_shape=jax.ShapeDtypeStruct((holders * PIECE, LANES), jnp.float32),
        in_specs=[VMEM, HBM],
        out_specs=VMEM,
        scratch_shapes=[
            pltpu.VMEM((3, owners, LANES), jnp.int32),
            pltpu.SMEM((3, owners, LANES), jnp.int32),
            pltpu.VMEM((NR, (BPT + 1) * LANES), jnp.float32),
            pltpu.VMEM((NR, NR), jnp.float32),
            pltpu.SemaphoreType.DMA((2,)),
        ],
        compiler_params=SMALL,
    )(arrived, in_hbm(radial_smoother))
    shells = lax.all_to_all(
        pieces.reshape(holders, 1, PIECE * LANES), "sp", split_axis=0, concat_axis=0, tiled=True
    ).reshape(holders * PIECE, LANES)
    padded = pltpu.VMEM((mine, rows + 2 * TILE, LANES), jnp.float32)
    plain = pltpu.VMEM((mine, rows, LANES), jnp.float32)
    side_rows = holders // SIDES * TILE
    side = pltpu.VMEM((side_rows + 2 * TILE, LANES), jnp.float32)
    return pl.pallas_call(
        functools.partial(diffuse_kernel, owners),
        out_shape=jax.ShapeDtypeStruct((mine, rows, columns // owners), jnp.float32),
        in_specs=[VMEM, HBM, VMEM],
        out_specs=HBM,
        scratch_shapes=[
            pltpu.SMEM((mine,), jnp.int32),
            padded,
            padded,
            side,
            side,
            pltpu.VMEM((side_rows, LANES), jnp.float32),
            plain,
            plain,
            plain,
            pltpu.VMEM((2 * LANES, LANES), jnp.bfloat16),
            pltpu.VMEM((2 * LANES, 2 * LANES), jnp.bfloat16),
            pltpu.VMEM((side_rows, LANES), jnp.float32),
            pltpu.SemaphoreType.DMA((SIDES + 1,)),
        ],
        compiler_params=SMALL,
    )(shells, in_hbm(shell_level), lateral_scale)


def solution(mesh):
    placed = (P("ev", None, "sp", None), P("ev", "sp"), P(), P("sp"), P())
    return jax.shard_map(
        per_device, mesh=mesh, in_specs=placed, out_specs=P("sp", None, "ev"), check_vma=False
    )
```

time: 79.9 us -> 73.6 us (0.921)
  Pallas kernels: 11.8 us -> 6.32 us
    pallas_call x1, Pallas kernels: 5.3 us -> 3.2 us  [per_device(): pl.pallas_call(functools.partial(diffuse_kernel, owners), out_shape=jax.S...]
    pallas_call x1, Pallas kernels: 3.71 us -> 1.69 us  [per_device(): pl.pallas_call(functools.partial(smooth_kernel, owners), out_shape=jax.Sh...]
    pallas_call x1, Pallas kernels: 2.81 us -> 1.43 us  [per_device(): pl.pallas_call(functools.partial(pack_kernel, owners), out_shape=jax.Shap...]
where the time goes in v2:
time: 73.6 us; the launch traced here: 73.4 us
  blocking collectives  67 us (91%)
  Pallas kernels  6.32 us (9%)
    all_to_all x1, blocking collectives, per_device(): lax.all_to_all(pieces.reshape(holders, 1, PIECE * LANES), 'sp', split_axi...  51.9 us
    all_to_all x1, blocking collectives, per_device(): lax.all_to_all(packed.reshape(owners, MESSAGE, LANES), 'ev', split_axis=0...  15.2 us
    pallas_call x1, Pallas kernels, per_device(): pl.pallas_call(functools.partial(diffuse_kernel, owners), out_shape=jax.S...  3.2 us
    pallas_call x1, Pallas kernels, per_device(): pl.pallas_call(functools.partial(smooth_kernel, owners), out_shape=jax.Sh...  1.69 us

profile of v2, /device:TPU:8, one launch (start us, length us, event | category | flops | bytes accessed | tf_op | source)
XLA Modules:
  0.0 73.4 jit_solution(13208400616805919947)
XLA Ops:
  0.0 0.0 copy-start
  0.0 1.4 %shard_map.55 = f32[576,128]{1,0:T(8,128)S(1)} custom-call(s32[1,8]{1,0:T(1,128)} %ids_hbm.1, f32[256,128]{1,0:T(8,128)} %bitcast.7), custom_call_target="tpu_custom_call" | custom-call | tf_op jit(solution)/shard_map/pallas_call | solution.py:332
  1.4 15.2 %all_to_all.10.arrived_ref = f32[8,72,128]{2,1,0:T(8,128)S(1)} all-to-all(f32[8,72,128]{2,1,0:T(8,128)S(1)} %bitcast.6), channel_id=1, replica_groups=mesh['ev'=8,'sp'=64] {'ev'}, dimensions={0} | all-to-all | bytes 589824 | tf_op jit(solution)/shard_map/all_to_all | solution.py:344
  16.6 1.7 %shard_map.56 = f32[1088,128]{1,0:T(8,128)S(1)} custom-call(f32[8,72,128]{2,1,0:T(8,128)S(1)} %all_to_all.10.arrived_ref, f32[128,128]{1,0:T(8,128)} %smoother_hbm.1), custom_call_target="tpu_custom_call" | custom-call | tf_op jit(solution)/shard_map/pallas_call | solution.py:347
  18.3 51.9 %all_to_all.11 = f32[64,1,2176]{2,1,0:T(1,128)S(1)} all-to-all(f32[64,1,2176]{2,1,0:T(1,128)S(1)} %bitcast.4), channel_id=1, replica_groups=mesh['ev'=8,'sp'=64] {'sp'}, dimensions={0} | all-to-all | bytes 1114112 | tf_op jit(solution)/shard_map/all_to_all | solution.py:361
  70.2 0.0 copy-done
  70.2 3.2 %shard_map.57 = f32[2,512,128]{2,1,0:T(8,128)} custom-call(f32[1088,128]{1,0:T(8,128)S(1)} %bitcast.5, s32[2]{0:T(128)} %level_hbm.1, f32[512,1024]{1,0:T(8,128)S(1)} %copy-done), custom_call_target="tpu_custom_call" | custom-call | tf_op jit(solution)/shard_map/pallas_call | solution.py:368
Async XLA Ops:
  0.0 70.2 %copy-start = (f32[512,1024]{1,0:T(8,128)S(1)}, f32[512,1024]{1,0:T(8,128)}, u32[]{:S(2)}) copy-start(f32[512,1024]{1,0:T(8,128)} %scale_ref.1) | copy-start | bytes 6291460

commit v3 on v2

v3 whole, which is shorter than its diff:
```python
import functools

import jax
import jax.numpy as jnp
from jax import lax
from jax.experimental import pallas as pl
from jax.experimental.pallas import tpu as pltpu
from jax.sharding import PartitionSpec as P

NR = 128
RB = 32
BY = 128
BPT = 8
CAP = 2
PASSES = 4
NSEG = 4
PER_OWNER = BPT * NSEG
LANES = 128
TILE = 8
MESSAGE = CAP * RB + TILE
LABELS = 64
STRIP = 16
SIDES = 4
PIECE = 2 * BPT + 1

diffusion_rate = 0.0615

SMALL = pltpu.CompilerParams(vmem_limit_bytes=12 * 1024 * 1024)
VMEM = pl.BlockSpec(memory_space=pltpu.VMEM)
HBM = pl.BlockSpec(memory_space=pltpu.HBM)


def lane_index(shape=(TILE, LANES)):
    return lax.broadcasted_iota(jnp.int32, shape, len(shape) - 1)


def stencil_matrices(near_ref, side_near_ref):
    row_of = lax.broadcasted_iota(jnp.int32, (LANES, LANES), 0)
    lane_of = lax.broadcasted_iota(jnp.int32, (LANES, LANES), 1)
    beside = jnp.abs(row_of - lane_of) == 1
    middle = jnp.where(row_of == lane_of, -4.0, 0.0)
    near = jnp.where(beside, 1.0, middle).astype(jnp.bfloat16)
    from_in, to_in = lax.bitwise_and(row_of, STRIP - 1), lax.bitwise_and(lane_of, STRIP - 1)
    same_strip = lax.shift_right_logical(row_of, 4) == lax.shift_right_logical(lane_of, 4)
    same_run = lax.shift_right_logical(row_of, 2) == lax.shift_right_logical(lane_of, 2)
    apart, later = jnp.abs(from_in - to_in), jnp.maximum(from_in, to_in)
    joined = ((apart == 7) & (later == 11)) | ((apart == 9) & (later == 12))
    side_near = jnp.where((beside & same_run) | (joined & same_strip), 1.0, middle).astype(jnp.bfloat16)
    exchanged = jnp.where(to_in == 11, lane_of + 1, jnp.where(to_in == 12, lane_of - 1, lane_of))
    exchange = jnp.where(row_of == exchanged, 1.0, 0.0).astype(jnp.bfloat16)
    for part in range(2):
        at = slice(part * LANES, (part + 1) * LANES)
        near_ref[at, :] = near
        side_near_ref[at, 0:LANES] = side_near
        side_near_ref[at, LANES:] = exchange


def pack_kernel(
    owners, ids_hbm, blocks_hbm, scale_hbm, out_ref, scale_ref, near_ref, side_near_ref,
    ids_ref, blocks_ref, sems,
):
    ids_copy = pltpu.make_async_copy(ids_hbm, ids_ref, sems.at[0])
    blocks_copy = pltpu.make_async_copy(blocks_hbm, blocks_ref, sems.at[1])
    ids_copy.start()
    blocks_copy.start()
    here = lax.axis_index("ev")
    width = scale_ref.shape[2]
    places = (jnp.maximum(here - 1, 0), here, jnp.minimum(here + 1, owners - 1))
    scale_copies = [
        pltpu.make_async_copy(
            scale_hbm.at[:, pl.ds(pl.multiple_of(place * width, width), width)],
            scale_ref.at[n],
            sems.at[2 + n],
        )
        for n, place in enumerate(places)
    ]
    for copy in scale_copies:
        copy.start()
    listed = ids_ref.shape[1]
    lane = lane_index()
    zero = jnp.zeros((TILE, LANES), jnp.float32)
    for row in range(0, owners * MESSAGE, TILE):
        out_ref[row : row + TILE, :] = zero
    stencil_matrices(near_ref, side_near_ref)
    ids_copy.wait()
    ids = [ids_ref[0, j] for j in range(listed)]
    owner_of = [lax.shift_right_logical(i, 5) for i in ids]
    ranks = []
    for j in range(listed):
        rank = jnp.int32(0)
        for i in range(j):
            rank = rank + jnp.where(owner_of[i] == owner_of[j], 1, 0)
        ranks.append(rank)
    blocks_copy.wait()

    def add(owner, cells):
        there = pl.ds(pl.multiple_of(owner * MESSAGE + CAP * RB, TILE), TILE)
        out_ref[there, :] = out_ref[there, :] + cells

    for j in range(listed):
        owner, rank = owner_of[j], ranks[j]
        within = lax.bitwise_and(ids[j], PER_OWNER - 1).astype(jnp.float32)
        first = zero
        last = zero
        for a in range(RB // TILE):
            cells = blocks_ref[pl.ds(a * TILE * listed + j, TILE, stride=listed), :]
            start = pl.multiple_of(owner * MESSAGE + rank * RB + a * TILE, TILE)
            out_ref[pl.ds(start, TILE), :] = cells
            head = jnp.where(lane < 4, cells, 0.0)
            tail = jnp.where(lane >= LANES - 4, cells, 0.0)
            first = first + (pltpu.roll(head, 16 * a, 1) if a else head)
            last = last + pltpu.roll(tail, 16 * a + 4, 1)
        add(owner, jnp.where(lane == LABELS + rank, within, 0.0))
        later = rank == 1
        to_left = jnp.where(later, pltpu.roll(first, 12, 1), pltpu.roll(first, 8, 1))
        to_left = to_left + jnp.where(lane == LABELS + 4 + rank, within, 0.0)
        to_right = jnp.where(later, pltpu.roll(last, 4, 1), last)
        to_right = to_right + jnp.where(lane == LABELS + 2 + rank, within, 0.0)
        add(jnp.maximum(owner - 1, 0), jnp.where(owner > 0, to_left, 0.0))
        add(jnp.minimum(owner + 1, owners - 1), jnp.where(owner < owners - 1, to_right, 0.0))
    for copy in scale_copies:
        copy.wait()


def halves(cells):
    high = cells.astype(jnp.bfloat16)
    low = (cells - high.astype(jnp.float32)).astype(jnp.bfloat16)
    return high, low


def scale_strips(scale_ref, owners):
    here = lax.axis_index("ev")
    part = scale_ref.shape[1] // SIDES
    lane = lane_index((part, LANES))
    inner = lax.bitwise_and(lane, STRIP - 1) < 8
    strip = lax.shift_right_logical(lane, 4)
    keep_after = (lane < 4) & (here < owners - 1)
    keep_before = (lane >= LANES - 4) & (here > 0)
    strips = jnp.zeros((part, LANES), jnp.float32)
    for n in range(SIDES):
        at = slice(n * part, (n + 1) * part)
        beyond = jnp.where(keep_before, scale_ref[0, at, :], 0.0)
        beyond = jnp.where(keep_after, scale_ref[2, at, :], beyond)
        both = jnp.where(
            inner,
            pltpu.roll(scale_ref[1, at, :], STRIP * n + 4, 1),
            pltpu.roll(beyond, STRIP * n + 12, 1),
        )
        strips = jnp.where(strip == n, both, strips)
    return strips + pltpu.roll(strips, LANES // 2, 1)


def smooth_kernel(
    groups, arrived_ref, scale_ref, smoother_hbm, out_ref, side_scale_ref,
    spots_ref, labels_ref, columns_ref, smoother_ref, sems,
):
    smoother_copy = pltpu.make_async_copy(smoother_hbm, smoother_ref, sems.at[1])
    smoother_copy.start()
    labels = arrived_ref[:, CAP * RB, :].astype(jnp.int32)
    rows = lax.shift_right_logical(labels, 2)
    label_lane = lane_index((groups, LANES)) - (LABELS + CAP)
    shift = jnp.where(label_lane >= CAP, 4, 0)
    spots_ref[0] = lax.bitwise_and(labels, NSEG - 1) * RB
    spots_ref[1] = rows * LANES
    spots_ref[2] = (BPT - 1 - rows) * 8 + shift
    labels_copy = pltpu.make_async_copy(spots_ref, labels_ref, sems.at[0])
    labels_copy.start()
    lane = lane_index()
    lane_four = lax.bitwise_and(lane, ~3)
    columns_ref[...] = jnp.zeros_like(columns_ref)
    side_scale_ref[...] = scale_strips(scale_ref, groups)
    labels_copy.wait()
    for g in range(groups):
        for rank in range(CAP):
            where = (
                pl.ds(pl.multiple_of(labels_ref[0, g, LABELS + rank], RB), RB),
                pl.ds(pl.multiple_of(labels_ref[1, g, LABELS + rank], LANES), LANES),
            )
            columns_ref[where] = columns_ref[where] + arrived_ref[g, rank * RB : (rank + 1) * RB, :]
    for g in range(groups):
        edges = arrived_ref[g, CAP * RB :, :]
        for h in range(2 * CAP):
            target = labels_ref[2, g, LABELS + CAP + h]
            keep = lane_four == target
            turned = pltpu.roll(edges, lax.bitwise_and(target + (LANES - 4 * h), LANES - 1), 1)
            parts = [turned] + [
                pltpu.roll(turned, LANES - 16 * a, 1) for a in range(1, RB // TILE)
            ]
            four = jnp.concatenate([jnp.where(keep, part, 0.0) for part in parts], axis=0)
            where = (
                pl.ds(pl.multiple_of(labels_ref[0, g, LABELS + CAP + h], RB), RB),
                pl.ds(BPT * LANES, LANES),
            )
            columns_ref[where] = columns_ref[where] + four
    edge_columns = columns_ref[:, BPT * LANES :]
    columns_ref[:, BPT * LANES :] = edge_columns + pltpu.roll(edge_columns, LANES // 2, 1)
    smoother_copy.wait()
    half = NR // 2
    smoother = jnp.concatenate(
        [smoother_ref[pl.ds(0, half, stride=2), :], smoother_ref[pl.ds(1, half, stride=2), :]], axis=0
    )
    high, low = halves(smoother)
    twice = jnp.concatenate([high, high], axis=1)

    def smoothed(start, width):
        first, second = halves(columns_ref[:, start : start + width])
        both = jnp.concatenate([first, second], axis=0)
        return jnp.dot(twice, both, preferred_element_type=jnp.float32) + jnp.dot(
            low, first, preferred_element_type=jnp.float32
        )

    for row in range(0, BPT, 2):
        done = smoothed(row * LANES, 2 * LANES)
        for i in range(2):
            cells = done[:, i * LANES : (i + 1) * LANES]
            out_ref[pl.ds(row + i, half, stride=PIECE), :] = cells[:half]
            out_ref[pl.ds(BPT + row + i, half, stride=PIECE), :] = cells[half:]
    done = smoothed(BPT * LANES, LANES)
    lower = lane_index((half, LANES)) < LANES // 2
    out_ref[pl.ds(2 * BPT, half, stride=PIECE), :] = jnp.where(lower, done[:half], done[half:])


def diffuse_kernel(
    cells_ref, level_hbm, scale_ref, side_scale_ref, near_ref, side_near_ref, out_hbm,
    level_ref, main_a, main_b, side_a, side_b, coefficient_ref, edge_ref, out_ref, sems,
):
    shells, rows, _ = out_ref.shape
    level_copy = pltpu.make_async_copy(level_hbm, level_ref, sems.at[SIDES])
    level_copy.start()
    nothing = jnp.zeros((TILE, LANES), jnp.float32)
    stripes = rows // BPT
    tiles = stripes // SIDES
    part = tiles * TILE
    for buffer in (main_a, main_b):
        for shell in range(shells):
            buffer[shell, 0:TILE, :] = nothing
            buffer[shell, TILE + rows : 2 * TILE + rows, :] = nothing
    slots = [(n, shell, (1 - shell) * SIDES + n) for n in range(SIDES) for shell in range(shells)]

    strip = lax.shift_right_logical(lane_index(), 4)
    for v in range(tiles):
        outer = nothing
        for n in range(SIDES):
            stripe = n * tiles + v
            at = stripe * PIECE
            spot = TILE + stripe * BPT
            wide = jnp.broadcast_to(cells_ref[at + 2 * BPT : at + PIECE, :], (TILE, LANES))
            turned = pltpu.roll(wide, STRIP * (n + 1), 1, stride=8, stride_axis=0)
            outer = jnp.where(lax.bitwise_and(strip, SIDES - 1) == n, turned, outer)
            for shell in range(shells):
                main_a[shell, spot : spot + BPT, :] = cells_ref[
                    at + shell * BPT : at + (shell + 1) * BPT, :
                ]
        side_a[TILE + v * TILE : 2 * TILE + v * TILE, :] = outer
    lane = lane_index((part, LANES))
    strip = lax.shift_right_logical(lane, 4)
    inner = lax.bitwise_and(lane, STRIP - 1) < 8
    side = side_a[TILE : TILE + part, :]
    for n, shell, slot in slots:
        cells = main_a[shell, TILE + n * part : TILE + (n + 1) * part, :]
        side = jnp.where(inner & (strip == slot), pltpu.roll(cells, STRIP * slot + 4, 1), side)
    side_a[TILE : TILE + part, :] = side

    lane_row = lane_index((1, LANES))
    stripe_in = lax.bitwise_and(lane_row, SIDES * STRIP - 1)
    last_row = TILE + part - 1

    def join(side):
        down = pltpu.roll(side[last_row : last_row + 1, :], STRIP, 1)
        side[TILE - 1 : TILE, :] = jnp.where(stripe_in < STRIP, 0.0, down)
        up = pltpu.roll(side[TILE : TILE + 1, :], LANES - STRIP, 1)
        side[last_row + 1 : last_row + 2, :] = jnp.where(stripe_in >= (SIDES - 1) * STRIP, 0.0, up)

    join(side_a)
    level_copy.wait()
    factors = [diffusion_rate * level_ref[shell].astype(jnp.float32) for shell in range(shells)]
    side_factor = jnp.where(lane < LANES // 2, factors[1], factors[0])
    is_edge = (lane == 0) | (lane == LANES - 1)

    def across(cells, matrix):
        return jnp.dot(
            jnp.concatenate(halves(cells), axis=1), matrix[...], preferred_element_type=jnp.float32
        )

    copies = []
    buffers = ((main_a, side_a), (main_b, side_b))
    for repeat in range(PASSES):
        (main, side), (main_next, side_next) = buffers[repeat % 2], buffers[(repeat + 1) % 2]
        final = repeat == PASSES - 1
        middle = side[TILE : TILE + part, :]
        sums = across(middle, side_near_ref)
        edge_ref[...] = sums[:, LANES:]
        if not final:
            vertical = side[TILE - 1 : TILE + part - 1, :] + side[TILE + 1 : TILE + part + 1, :]
            coefficient = side_factor * side_scale_ref[...]
            side_next[TILE : TILE + part, :] = middle + coefficient * (vertical + sums[:, :LANES])
            join(side_next)
        for n, shell, slot in slots:
            at = slice(n * part, (n + 1) * part)
            first = TILE + n * part
            middle = main[shell, first : first + part, :]
            sums = across(middle, near_ref)
            turned = pltpu.roll(edge_ref[...], (2 * LANES - STRIP * slot - 12) % LANES, 1)
            vertical = (
                main[shell, first - 1 : first + part - 1, :]
                + main[shell, first + 1 : first + part + 1, :]
            )
            if repeat == 0:
                coefficient = factors[shell] * scale_ref[1, at, :]
                coefficient_ref[shell, at, :] = coefficient
            else:
                coefficient = coefficient_ref[shell, at, :]
            new = middle + coefficient * ((vertical + sums) + jnp.where(is_edge, turned, 0.0))
            if not final:
                main_next[shell, first : first + part, :] = new
                continue
            out_ref[shell, at, :] = new
            if shell == shells - 1:
                done = pl.ds(n * part, part)
                copy = pltpu.make_async_copy(out_ref.at[:, done, :], out_hbm.at[:, done, :], sems.at[n])
                copy.start()
                copies.append(copy)
    for copy in copies:
        copy.wait()


def in_hbm(array):
    return pltpu.with_memory_space_constraint(array, pltpu.HBM)


def per_device(partial_kernels, block_ids, radial_smoother, shell_level, lateral_scale):
    owners = lax.axis_size("ev")
    holders = lax.axis_size("sp")
    listed = block_ids.shape[1]
    rows, columns = lateral_scale.shape
    mine = shell_level.shape[0]
    part = rows // SIDES
    packed, scale, near, side_near = pl.pallas_call(
        functools.partial(pack_kernel, owners),
        out_shape=[
            jax.ShapeDtypeStruct((owners * MESSAGE, LANES), jnp.float32),
            jax.ShapeDtypeStruct((3, rows, columns // owners), jnp.float32),
            jax.ShapeDtypeStruct((2 * LANES, LANES), jnp.bfloat16),
            jax.ShapeDtypeStruct((2 * LANES, 2 * LANES), jnp.bfloat16),
        ],
        in_specs=[HBM, HBM, HBM],
        out_specs=[VMEM, VMEM, VMEM, VMEM],
        scratch_shapes=[
            pltpu.SMEM((1, listed), jnp.int32),
            pltpu.VMEM((RB * listed, LANES), jnp.float32),
            pltpu.SemaphoreType.DMA((5,)),
        ],
        compiler_params=SMALL,
    )(
        in_hbm(block_ids),
        in_hbm(partial_kernels.reshape(RB * listed, BY)),
        in_hbm(lateral_scale),
    )
    arrived = lax.all_to_all(
        packed.reshape(owners, MESSAGE, LANES), "ev", split_axis=0, concat_axis=0, tiled=True
    )
    pieces, side_scale = pl.pallas_call(
        functools.partial(smooth_kernel, owners),
        out_shape=[
            jax.ShapeDtypeStruct((holders * PIECE, LANES), jnp.float32),
            jax.ShapeDtypeStruct((part, LANES), jnp.float32),
        ],
        in_specs=[VMEM, VMEM, HBM],
        out_specs=[VMEM, VMEM],
        scratch_shapes=[
            pltpu.VMEM((3, owners, LANES), jnp.int32),
            pltpu.SMEM((3, owners, LANES), jnp.int32),
            pltpu.VMEM((NR, (BPT + 1) * LANES), jnp.float32),
            pltpu.VMEM((NR, NR), jnp.float32),
            pltpu.SemaphoreType.DMA((2,)),
        ],
        compiler_params=SMALL,
    )(arrived, scale, in_hbm(radial_smoother))
    shells = lax.all_to_all(
        pieces.reshape(holders, 1, PIECE * LANES), "sp", split_axis=0, concat_axis=0, tiled=True
    ).reshape(holders * PIECE, LANES)
    padded = pltpu.VMEM((mine, rows + 2 * TILE, LANES), jnp.float32)
    plain = pltpu.VMEM((mine, rows, LANES), jnp.float32)
    side = pltpu.VMEM((part + 2 * TILE, LANES), jnp.float32)
    return pl.pallas_call(
        diffuse_kernel,
        out_shape=jax.ShapeDtypeStruct((mine, rows, columns // owners), jnp.float32),
        in_specs=[VMEM, HBM, VMEM, VMEM, VMEM, VMEM],
        out_specs=HBM,
        scratch_shapes=[
            pltpu.SMEM((mine,), jnp.int32),
            padded,
            padded,
            side,
            side,
            plain,
            pltpu.VMEM((part, LANES), jnp.float32),
            plain,
            pltpu.SemaphoreType.DMA((SIDES + 1,)),
        ],
        compiler_params=SMALL,
    )(shells, in_hbm(shell_level), scale, side_scale, near, side_near)


def solution(mesh):
    placed = (P("ev", None, "sp", None), P("ev", "sp"), P(), P("sp"), P())
    return jax.shard_map(
        per_device, mesh=mesh, in_specs=placed, out_specs=P("sp", None, "ev"), check_vma=False
    )
```

time: 73.6 us -> 73 us (level)
  no operation moved by 1% of the time
where the time goes in v3:
time: 73 us; the launch traced here: 72.8 us
  blocking collectives  67 us (92%)
  Pallas kernels  5.73 us (8%)
    all_to_all x1, blocking collectives, per_device(): lax.all_to_all(pieces.reshape(holders, 1, PIECE * LANES), 'sp', split_axi...  51.9 us
    all_to_all x1, blocking collectives, per_device(): lax.all_to_all(packed.reshape(owners, MESSAGE, LANES), 'ev', split_axis=0...  15.2 us
    pallas_call x1, Pallas kernels, per_device(): pl.pallas_call(diffuse_kernel, out_shape=jax.ShapeDtypeStruct((mine, rows...  2.55 us
    pallas_call x1, Pallas kernels, per_device(): pl.pallas_call(functools.partial(smooth_kernel, owners), out_shape=[jax.S...  1.87 us

profile of v3, /device:TPU:8, one launch (start us, length us, event | category | flops | bytes accessed | tf_op | source)
XLA Modules:
  0.0 72.8 jit_solution(7301235161932493348)
XLA Ops:
  0.0 1.3 %shard_map.55 = (f32[576,128]{1,0:T(8,128)S(1)}, f32[3,512,128]{2,1,0:T(8,128)S(1)}, bf16[256,128]{1,0:T(8,128)(2,1)S(1)}, bf16[256,256]{1,0:T(8,128)(2,1)S(1)}) custom-call(s32[1,8]{1,0:T(1,128)} %ids_hbm.1, f32[256,128]{1,0:T(8,128)} %bitcast.7, f32[512,1024]{1,0:T(8,128)} %scale_hbm.1), custom_call_target="tpu_custom_call" | custom-call | tf_op jit(solution)/shard_map/pallas_call | solution.py:338
  1.3 15.2 %all_to_all.10.arrived_ref = f32[8,72,128]{2,1,0:T(8,128)S(1)} all-to-all(f32[8,72,128]{2,1,0:T(8,128)S(1)} %bitcast.6), channel_id=1, replica_groups=mesh['ev'=8,'sp'=64] {'ev'}, dimensions={0} | all-to-all | bytes 589824 | tf_op jit(solution)/shard_map/all_to_all | solution.py:359
  16.5 1.9 %shard_map.56 = (f32[1088,128]{1,0:T(8,128)S(1)}, f32[128,128]{1,0:T(8,128)S(1)}) custom-call(f32[8,72,128]{2,1,0:T(8,128)S(1)} %all_to_all.10.arrived_ref, f32[3,512,128]{2,1,0:T(8,128)S(1)} %get-tuple-element.12.scale_ref, f32[128,128]{1,0:T(8,128)} %smoother_hbm.1), custom_call_target="tpu_custom_call" | custom-call | tf_op jit(solution)/shard_map/pallas_call | solution.py:362
  18.4 51.9 %all_to_all.11 = f32[64,1,2176]{2,1,0:T(1,128)S(1)} all-to-all(f32[64,1,2176]{2,1,0:T(1,128)S(1)} %bitcast.5), channel_id=1, replica_groups=mesh['ev'=8,'sp'=64] {'sp'}, dimensions={0} | all-to-all | bytes 1114112 | tf_op jit(solution)/shard_map/all_to_all | solution.py:379
  70.2 2.6 %shard_map.57 = f32[2,512,128]{2,1,0:T(8,128)} custom-call(f32[1088,128]{1,0:T(8,128)S(1)} %bitcast.4, s32[2]{0:T(128)} %level_hbm.1, f32[3,512,128]{2,1,0:T(8,128)S(1)} %get-tuple-element.12.scale_ref, f32[128,128]{1,0:T(8,128)S(1)} %get-tuple-element.14.side_scale_ref, bf16[256,128]{1,0:T(8,128)(2,1)S(1)} %get-tuple-element.15.near_ref, ...), custom_call_target="tpu_custom_call" | custom-call | tf_op jit(solution)/shard_map/pallas_call | solution.py:385

commit v4 on v3

--- a/solution.py
+++ b/solution.py
@@ -56,8 +56,9 @@
 
 
 def pack_kernel(
-    owners, ids_hbm, blocks_hbm, scale_hbm, out_ref, scale_ref, near_ref, side_near_ref,
-    ids_ref, blocks_ref, sems,
+    owners, ids_hbm, blocks_hbm, scale_hbm, smoother_hbm, level_hbm,
+    out_ref, scale_ref, smoother_ref, factor_ref, near_ref, side_near_ref,
+    ids_ref, blocks_ref, level_ref, sems,
 ):
     ids_copy = pltpu.make_async_copy(ids_hbm, ids_ref, sems.at[0])
     blocks_copy = pltpu.make_async_copy(blocks_hbm, blocks_ref, sems.at[1])
@@ -66,7 +67,7 @@
     here = lax.axis_index("ev")
     width = scale_ref.shape[2]
     places = (jnp.maximum(here - 1, 0), here, jnp.minimum(here + 1, owners - 1))
-    scale_copies = [
+    copies = [
         pltpu.make_async_copy(
             scale_hbm.at[:, pl.ds(pl.multiple_of(place * width, width), width)],
             scale_ref.at[n],
@@ -74,7 +75,9 @@
         )
         for n, place in enumerate(places)
     ]
-    for copy in scale_copies:
+    copies.append(pltpu.make_async_copy(smoother_hbm, smoother_ref, sems.at[5]))
+    copies.append(pltpu.make_async_copy(level_hbm, level_ref, sems.at[6]))
+    for copy in copies:
         copy.start()
     listed = ids_ref.shape[1]
     lane = lane_index()
@@ -118,8 +121,11 @@
         to_right = to_right + jnp.where(lane == LABELS + 2 + rank, within, 0.0)
         add(jnp.maximum(owner - 1, 0), jnp.where(owner > 0, to_left, 0.0))
         add(jnp.minimum(owner + 1, owners - 1), jnp.where(owner < owners - 1, to_right, 0.0))
-    for copy in scale_copies:
+    for copy in copies:
         copy.wait()
+    for shell in range(level_ref.shape[0]):
+        factor = diffusion_rate * level_ref[shell].astype(jnp.float32)
+        factor_ref[shell] = jnp.full((TILE, LANES), factor, jnp.float32)
 
 
 def halves(cells):
@@ -151,23 +157,23 @@
 
 
 def smooth_kernel(
-    groups, arrived_ref, scale_ref, smoother_hbm, out_ref, side_scale_ref,
-    spots_ref, labels_ref, columns_ref, smoother_ref, sems,
+    groups, arrived_ref, scale_ref, smoother_ref, out_ref, side_scale_ref,
+    spots_ref, labels_ref, columns_ref, edge_ref, sems,
 ):
-    smoother_copy = pltpu.make_async_copy(smoother_hbm, smoother_ref, sems.at[1])
-    smoother_copy.start()
     labels = arrived_ref[:, CAP * RB, :].astype(jnp.int32)
     rows = lax.shift_right_logical(labels, 2)
+    segments = lax.bitwise_and(labels, NSEG - 1)
     label_lane = lane_index((groups, LANES)) - (LABELS + CAP)
-    shift = jnp.where(label_lane >= CAP, 4, 0)
-    spots_ref[0] = lax.bitwise_and(labels, NSEG - 1) * RB
+    spots_ref[0] = segments * jnp.where(label_lane >= 0, 2 * TILE, RB)
     spots_ref[1] = rows * LANES
-    spots_ref[2] = (BPT - 1 - rows) * 8 + shift
+    spots_ref[2] = (BPT - 1 - rows) * 8 + jnp.where(label_lane >= CAP, 4, 0)
     labels_copy = pltpu.make_async_copy(spots_ref, labels_ref, sems.at[0])
     labels_copy.start()
     lane = lane_index()
-    lane_four = lax.bitwise_and(lane, ~3)
-    columns_ref[...] = jnp.zeros_like(columns_ref)
+    low = lane < LANES // 2
+    lane_four = lax.bitwise_and(lane, LANES // 2 - 4)
+    columns_ref[:, : BPT * LANES] = jnp.zeros((NR, BPT * LANES), jnp.float32)
+    edge_ref[...] = jnp.zeros_like(edge_ref)
     side_scale_ref[...] = scale_strips(scale_ref, groups)
     labels_copy.wait()
     for g in range(groups):
@@ -179,34 +185,37 @@
             columns_ref[where] = columns_ref[where] + arrived_ref[g, rank * RB : (rank + 1) * RB, :]
     for g in range(groups):
         edges = arrived_ref[g, CAP * RB :, :]
+        pairs = [
+            jnp.where(low, edges, pltpu.roll(edges, 48, 1)),
+            jnp.where(low, pltpu.roll(edges, LANES - 32, 1), pltpu.roll(edges, 16, 1)),
+        ]
         for h in range(2 * CAP):
             target = labels_ref[2, g, LABELS + CAP + h]
             keep = lane_four == target
-            turned = pltpu.roll(edges, lax.bitwise_and(target + (LANES - 4 * h), LANES - 1), 1)
-            parts = [turned] + [
-                pltpu.roll(turned, LANES - 16 * a, 1) for a in range(1, RB // TILE)
-            ]
-            four = jnp.concatenate([jnp.where(keep, part, 0.0) for part in parts], axis=0)
-            where = (
-                pl.ds(pl.multiple_of(labels_ref[0, g, LABELS + CAP + h], RB), RB),
-                pl.ds(BPT * LANES, LANES),
+            shift = lax.bitwise_and(target + (LANES - 4 * h), LANES - 1)
+            four = jnp.concatenate(
+                [jnp.where(keep, pltpu.roll(pair, shift, 1), 0.0) for pair in pairs], axis=0
             )
-            columns_ref[where] = columns_ref[where] + four
-    edge_columns = columns_ref[:, BPT * LANES :]
-    columns_ref[:, BPT * LANES :] = edge_columns + pltpu.roll(edge_columns, LANES // 2, 1)
-    smoother_copy.wait()
+            where = pl.ds(pl.multiple_of(labels_ref[0, g, LABELS + CAP + h], 2 * TILE), 2 * TILE)
+            edge_ref[where, :] = edge_ref[where, :] + four
+    for pair in range(NR // (2 * TILE)):
+        cells = edge_ref[pair * TILE : (pair + 1) * TILE, :]
+        turned = pltpu.roll(cells, LANES // 2, 1)
+        at = pair * 2 * TILE
+        columns_ref[at : at + TILE, BPT * LANES :] = jnp.where(low, cells, turned)
+        columns_ref[at + TILE : at + 2 * TILE, BPT * LANES :] = jnp.where(low, turned, cells)
     half = NR // 2
     smoother = jnp.concatenate(
         [smoother_ref[pl.ds(0, half, stride=2), :], smoother_ref[pl.ds(1, half, stride=2), :]], axis=0
     )
-    high, low = halves(smoother)
+    high, rest = halves(smoother)
     twice = jnp.concatenate([high, high], axis=1)
 
     def smoothed(start, width):
         first, second = halves(columns_ref[:, start : start + width])
         both = jnp.concatenate([first, second], axis=0)
         return jnp.dot(twice, both, preferred_element_type=jnp.float32) + jnp.dot(
-            low, first, preferred_element_type=jnp.float32
+            rest, first, preferred_element_type=jnp.float32
         )
 
     for row in range(0, BPT, 2):
@@ -221,12 +230,10 @@
 
 
 def diffuse_kernel(
-    cells_ref, level_hbm, scale_ref, side_scale_ref, near_ref, side_near_ref, out_hbm,
-    level_ref, main_a, main_b, side_a, side_b, coefficient_ref, edge_ref, out_ref, sems,
+    cells_ref, factor_ref, scale_ref, side_scale_ref, near_ref, side_near_ref, out_hbm,
+    main_a, main_b, side_a, side_b, coefficient_ref, edge_ref, out_ref, sems,
 ):
     shells, rows, _ = out_ref.shape
-    level_copy = pltpu.make_async_copy(level_hbm, level_ref, sems.at[SIDES])
-    level_copy.start()
     nothing = jnp.zeros((TILE, LANES), jnp.float32)
     stripes = rows // BPT
     tiles = stripes // SIDES
@@ -255,11 +262,6 @@
     lane = lane_index((part, LANES))
     strip = lax.shift_right_logical(lane, 4)
     inner = lax.bitwise_and(lane, STRIP - 1) < 8
-    side = side_a[TILE : TILE + part, :]
-    for n, shell, slot in slots:
-        cells = main_a[shell, TILE + n * part : TILE + (n + 1) * part, :]
-        side = jnp.where(inner & (strip == slot), pltpu.roll(cells, STRIP * slot + 4, 1), side)
-    side_a[TILE : TILE + part, :] = side
 
     lane_row = lane_index((1, LANES))
     stripe_in = lax.bitwise_and(lane_row, SIDES * STRIP - 1)
@@ -271,35 +273,41 @@
         up = pltpu.roll(side[TILE : TILE + 1, :], LANES - STRIP, 1)
         side[last_row + 1 : last_row + 2, :] = jnp.where(stripe_in >= (SIDES - 1) * STRIP, 0.0, up)
 
-    join(side_a)
-    level_copy.wait()
-    factors = [diffusion_rate * level_ref[shell].astype(jnp.float32) for shell in range(shells)]
-    side_factor = jnp.where(lane < LANES // 2, factors[1], factors[0])
+    lane_tile = lane_index()
+    factors = [jnp.tile(factor_ref[shell], (tiles, 1)) for shell in range(shells)]
+    side_factor = jnp.tile(
+        jnp.where(lane_tile < LANES // 2, factor_ref[1], factor_ref[0]), (tiles, 1)
+    )
     is_edge = (lane == 0) | (lane == LANES - 1)
 
     def across(cells, matrix):
         return jnp.dot(
-            jnp.concatenate(halves(cells), axis=1), matrix[...], preferred_element_type=jnp.float32
+            jnp.concatenate(halves(cells), axis=1), matrix, preferred_element_type=jnp.float32
         )
+
+    def side_step(side, side_next, sums):
+        middle = side[TILE : TILE + part, :]
+        vertical = side[TILE - 1 : TILE + part - 1, :] + side[TILE + 1 : TILE + part + 1, :]
+        coefficient = side_factor * side_scale_ref[...]
+        side_next[TILE : TILE + part, :] = middle + coefficient * (vertical + sums)
+        join(side_next)
 
     copies = []
     buffers = ((main_a, side_a), (main_b, side_b))
     for repeat in range(PASSES):
         (main, side), (main_next, side_next) = buffers[repeat % 2], buffers[(repeat + 1) % 2]
         final = repeat == PASSES - 1
-        middle = side[TILE : TILE + part, :]
-        sums = across(middle, side_near_ref)
-        edge_ref[...] = sums[:, LANES:]
-        if not final:
-            vertical = side[TILE - 1 : TILE + part - 1, :] + side[TILE + 1 : TILE + part + 1, :]
-            coefficient = side_factor * side_scale_ref[...]
-            side_next[TILE : TILE + part, :] = middle + coefficient * (vertical + sums[:, :LANES])
-            join(side_next)
+        if repeat == 0 or final:
+            edge_ref[...] = across(side[TILE : TILE + part, :], side_near_ref[:, LANES:])
+        else:
+            sums = across(side[TILE : TILE + part, :], side_near_ref[...])
+            edge_ref[...] = sums[:, LANES:]
+            side_step(side, side_next, sums[:, :LANES])
         for n, shell, slot in slots:
             at = slice(n * part, (n + 1) * part)
             first = TILE + n * part
             middle = main[shell, first : first + part, :]
-            sums = across(middle, near_ref)
+            sums = across(middle, near_ref[...])
             turned = pltpu.roll(edge_ref[...], (2 * LANES - STRIP * slot - 12) % LANES, 1)
             vertical = (
                 main[shell, first - 1 : first + part - 1, :]
@@ -308,6 +316,11 @@
             if repeat == 0:
                 coefficient = factors[shell] * scale_ref[1, at, :]
                 coefficient_ref[shell, at, :] = coefficient
+                side[TILE : TILE + part, :] = jnp.where(
+                    inner & (strip == slot),
+                    pltpu.roll(middle, STRIP * slot + 4, 1),
+                    side[TILE : TILE + part, :],
+                )
             else:
                 coefficient = coefficient_ref[shell, at, :]
             new = middle + coefficient * ((vertical + sums) + jnp.where(is_edge, turned, 0.0))
@@ -320,6 +333,11 @@
                 copy = pltpu.make_async_copy(out_ref.at[:, done, :], out_hbm.at[:, done, :], sems.at[n])
                 copy.start()
                 copies.append(copy)
+        if repeat == 0:
+            join(side)
+            side_step(
+                side, side_next, across(side[TILE : TILE + part, :], side_near_ref[:, :LANES])
+            )
     for copy in copies:
         copy.wait()
 
@@ -335,26 +353,31 @@
     rows, columns = lateral_scale.shape
     mine = shell_level.shape[0]
     part = rows // SIDES
-    packed, scale, near, side_near = pl.pallas_call(
+    packed, scale, smoother, factor, near, side_near = pl.pallas_call(
         functools.partial(pack_kernel, owners),
         out_shape=[
             jax.ShapeDtypeStruct((owners * MESSAGE, LANES), jnp.float32),
             jax.ShapeDtypeStruct((3, rows, columns // owners), jnp.float32),
+            jax.ShapeDtypeStruct((NR, NR), jnp.float32),
+            jax.ShapeDtypeStruct((mine, TILE, LANES), jnp.float32),
             jax.ShapeDtypeStruct((2 * LANES, LANES), jnp.bfloat16),
             jax.ShapeDtypeStruct((2 * LANES, 2 * LANES), jnp.bfloat16),
         ],
-        in_specs=[HBM, HBM, HBM],
-        out_specs=[VMEM, VMEM, VMEM, VMEM],
+        in_specs=[HBM] * 5,
+        out_specs=[VMEM] * 6,
         scratch_shapes=[
             pltpu.SMEM((1, listed), jnp.int32),
             pltpu.VMEM((RB * listed, LANES), jnp.float32),
-            pltpu.SemaphoreType.DMA((5,)),
+            pltpu.SMEM((mine,), jnp.int32),
+            pltpu.SemaphoreType.DMA((7,)),
         ],
         compiler_params=SMALL,
     )(
         in_hbm(block_ids),
         in_hbm(partial_kernels.reshape(RB * listed, BY)),
         in_hbm(lateral_scale),
+        in_hbm(radial_smoother),
+        in_hbm(shell_level),
     )
     arrived = lax.all_to_all(
         packed.reshape(owners, MESSAGE, LANES), "ev", split_axis=0, concat_axis=0, tiled=True
@@ -365,17 +388,17 @@
             jax.ShapeDtypeStruct((holders * PIECE, LANES), jnp.float32),
             jax.ShapeDtypeStruct((part, LANES), jnp.float32),
         ],
-        in_specs=[VMEM, VMEM, HBM],
-        out_specs=[VMEM, VMEM],
+        in_specs=[VMEM] * 3,
+        out_specs=[VMEM] * 2,
         scratch_shapes=[
             pltpu.VMEM((3, owners, LANES), jnp.int32),
             pltpu.SMEM((3, owners, LANES), jnp.int32),
             pltpu.VMEM((NR, (BPT + 1) * LANES), jnp.float32),
-            pltpu.VMEM((NR, NR), jnp.float32),
-            pltpu.SemaphoreType.DMA((2,)),
+            pltpu.VMEM((NR // 2, LANES), jnp.float32),
+            pltpu.SemaphoreType.DMA((1,)),
         ],
         compiler_params=SMALL,
-    )(arrived, scale, in_hbm(radial_smoother))
+    )(arrived, scale, smoother)
     shells = lax.all_to_all(
         pieces.reshape(holders, 1, PIECE * LANES), "sp", split_axis=0, concat_axis=0, tiled=True
     ).reshape(holders * PIECE, LANES)
@@ -385,10 +408,9 @@
     return pl.pallas_call(
         diffuse_kernel,
         out_shape=jax.ShapeDtypeStruct((mine, rows, columns // owners), jnp.float32),
-        in_specs=[VMEM, HBM, VMEM, VMEM, VMEM, VMEM],
+        in_specs=[VMEM] * 6,
         out_specs=HBM,
         scratch_shapes=[
-            pltpu.SMEM((mine,), jnp.int32),
             padded,
             padded,
             side,
@@ -396,10 +418,10 @@
             plain,
             pltpu.VMEM((part, LANES), jnp.float32),
             plain,
-            pltpu.SemaphoreType.DMA((SIDES + 1,)),
+            pltpu.SemaphoreType.DMA((SIDES,)),
         ],
         compiler_params=SMALL,
-    )(shells, in_hbm(shell_level), scale, side_scale, near, side_near)
+    )(shells, factor, scale, side_scale, near, side_near)
 
 
 def solution(mesh):

time: 73 us -> 72.3 us (level)
  no operation moved by 1% of the time
where the time goes in v4:
time: 72.3 us; the launch traced here: 72.1 us
  blocking collectives  67 us (93%)
  Pallas kernels  5.06 us (7%)
    all_to_all x1, blocking collectives, per_device(): lax.all_to_all(pieces.reshape(holders, 1, PIECE * LANES), 'sp', split_axi...  51.9 us
    all_to_all x1, blocking collectives, per_device(): lax.all_to_all(packed.reshape(owners, MESSAGE, LANES), 'ev', split_axis=0...  15.2 us
    pallas_call x1, Pallas kernels, per_device(): pl.pallas_call(diffuse_kernel, out_shape=jax.ShapeDtypeStruct((mine, rows...  2.05 us
    pallas_call x1, Pallas kernels, per_device(): pl.pallas_call(functools.partial(smooth_kernel, owners), out_shape=[jax.S...  1.66 us

profile of v4, /device:TPU:8, one launch (start us, length us, event | category | flops | bytes accessed | tf_op | source)
XLA Modules:
  0.0 72.1 jit_solution(8372143939942570692)
XLA Ops:
  0.0 1.3 %shard_map.55 = (f32[576,128]{1,0:T(8,128)S(1)}, f32[3,512,128]{2,1,0:T(8,128)S(1)}, f32[128,128]{1,0:T(8,128)S(1)}, f32[2,8,128]{2,1,0:T(8,128)S(1)}, bf16[256,...) custom-call(s32[1,8]{1,0:T(1,128)} %ids_hbm.1, f32[256,128]{1,0:T(8,128)} %bitcast.7, f32[512,1024]{1,0:T(8,128)} %scale_hbm.1, ...), custom_call_target="tpu_custom_call" | custom-call | tf_op jit(solution)/shard_map/pallas_call | solution.py:356
  1.4 15.2 %all_to_all.10.arrived_ref = f32[8,72,128]{2,1,0:T(8,128)S(1)} all-to-all(f32[8,72,128]{2,1,0:T(8,128)S(1)} %bitcast.6), channel_id=1, replica_groups=mesh['ev'=8,'sp'=64] {'ev'}, dimensions={0} | all-to-all | bytes 589824 | tf_op jit(solution)/shard_map/all_to_all | solution.py:382
  16.5 1.7 %shard_map.56 = (f32[1088,128]{1,0:T(8,128)S(1)}, f32[128,128]{1,0:T(8,128)S(1)}) custom-call(f32[8,72,128]{2,1,0:T(8,128)S(1)} %all_to_all.10.arrived_ref, f32[3,512,128]{2,1,0:T(8,128)S(1)} %get-tuple-element.14.scale_ref, f32[128,128]{1,0:T(8,128)S(1)} %get-tuple-element.15.smoother_ref), custom_call_target="tpu_custom_call" | custom-call | tf_op jit(solution)/shard_map/pallas_call | solution.py:385
  18.2 51.9 %all_to_all.11 = f32[64,1,2176]{2,1,0:T(1,128)S(1)} all-to-all(f32[64,1,2176]{2,1,0:T(1,128)S(1)} %bitcast.5), channel_id=1, replica_groups=mesh['ev'=8,'sp'=64] {'sp'}, dimensions={0} | all-to-all | bytes 1114112 | tf_op jit(solution)/shard_map/all_to_all | solution.py:402
  70.1 2.0 %shard_map.57 = f32[2,512,128]{2,1,0:T(8,128)} custom-call(f32[1088,128]{1,0:T(8,128)S(1)} %bitcast.4, f32[2,8,128]{2,1,0:T(8,128)S(1)} %get-tuple-element.17.factor_ref, f32[3,512,128]{2,1,0:T(8,128)S(1)} %get-tuple-element.14.scale_ref, f32[128,128]{1,0:T(8,128)S(1)} %get-tuple-element.18.side_scale_ref, bf16[256,128]{1,0:T(8,128)(2,1)S(1)} %get-tuple-element.19.near_ref, ...), custom_call_target="tpu_custom_call" | custom-call | tf_op jit(solution)/shard_map/pallas_call | solution.py:408

commit v5 on v4

--- a/solution.py
+++ b/solution.py
@@ -158,29 +158,26 @@
 
 def smooth_kernel(
     groups, arrived_ref, scale_ref, smoother_ref, out_ref, side_scale_ref,
-    spots_ref, labels_ref, columns_ref, edge_ref, sems,
+    columns_ref, edge_ref,
 ):
     labels = arrived_ref[:, CAP * RB, :].astype(jnp.int32)
-    rows = lax.shift_right_logical(labels, 2)
-    segments = lax.bitwise_and(labels, NSEG - 1)
-    label_lane = lane_index((groups, LANES)) - (LABELS + CAP)
-    spots_ref[0] = segments * jnp.where(label_lane >= 0, 2 * TILE, RB)
-    spots_ref[1] = rows * LANES
-    spots_ref[2] = (BPT - 1 - rows) * 8 + jnp.where(label_lane >= CAP, 4, 0)
-    labels_copy = pltpu.make_async_copy(spots_ref, labels_ref, sems.at[0])
-    labels_copy.start()
+    spots = [
+        [labels[g : g + 1, LABELS + i : LABELS + i + 1][0, 0] for i in range(3 * CAP)]
+        for g in range(groups)
+    ]
+    rows = [[lax.shift_right_logical(spot, 2) for spot in group] for group in spots]
+    segments = [[lax.bitwise_and(spot, NSEG - 1) for spot in group] for group in spots]
     lane = lane_index()
     low = lane < LANES // 2
     lane_four = lax.bitwise_and(lane, LANES // 2 - 4)
     columns_ref[:, : BPT * LANES] = jnp.zeros((NR, BPT * LANES), jnp.float32)
     edge_ref[...] = jnp.zeros_like(edge_ref)
     side_scale_ref[...] = scale_strips(scale_ref, groups)
-    labels_copy.wait()
     for g in range(groups):
         for rank in range(CAP):
             where = (
-                pl.ds(pl.multiple_of(labels_ref[0, g, LABELS + rank], RB), RB),
-                pl.ds(pl.multiple_of(labels_ref[1, g, LABELS + rank], LANES), LANES),
+                pl.ds(pl.multiple_of(segments[g][rank] * RB, RB), RB),
+                pl.ds(pl.multiple_of(rows[g][rank] * LANES, LANES), LANES),
             )
             columns_ref[where] = columns_ref[where] + arrived_ref[g, rank * RB : (rank + 1) * RB, :]
     for g in range(groups):
@@ -190,13 +187,13 @@
             jnp.where(low, pltpu.roll(edges, LANES - 32, 1), pltpu.roll(edges, 16, 1)),
         ]
         for h in range(2 * CAP):
-            target = labels_ref[2, g, LABELS + CAP + h]
+            target = (BPT - 1 - rows[g][CAP + h]) * 8 + (4 if h >= CAP else 0)
             keep = lane_four == target
             shift = lax.bitwise_and(target + (LANES - 4 * h), LANES - 1)
             four = jnp.concatenate(
                 [jnp.where(keep, pltpu.roll(pair, shift, 1), 0.0) for pair in pairs], axis=0
             )
-            where = pl.ds(pl.multiple_of(labels_ref[0, g, LABELS + CAP + h], 2 * TILE), 2 * TILE)
+            where = pl.ds(pl.multiple_of(segments[g][CAP + h] * (2 * TILE), 2 * TILE), 2 * TILE)
             edge_ref[where, :] = edge_ref[where, :] + four
     for pair in range(NR // (2 * TILE)):
         cells = edge_ref[pair * TILE : (pair + 1) * TILE, :]
@@ -391,11 +388,8 @@
         in_specs=[VMEM] * 3,
         out_specs=[VMEM] * 2,
         scratch_shapes=[
-            pltpu.VMEM((3, owners, LANES), jnp.int32),
-            pltpu.SMEM((3, owners, LANES), jnp.int32),
             pltpu.VMEM((NR, (BPT + 1) * LANES), jnp.float32),
             pltpu.VMEM((NR // 2, LANES), jnp.float32),
-            pltpu.SemaphoreType.DMA((1,)),
         ],
         compiler_params=SMALL,
     )(arrived, scale, smoother)

time: 72.3 us -> 71.4 us (0.988)
  Pallas kernels: 5.06 us -> 4.18 us
    pallas_call x1, Pallas kernels: 1.66 us -> 0.79 us  [per_device(): pl.pallas_call(functools.partial(smooth_kernel, owners), out_shape=[jax.S...]
where the time goes in v5:
time: 71.4 us; the launch traced here: 71.2 us
  blocking collectives  67 us (94%)
  Pallas kernels  4.18 us (6%)
    all_to_all x1, blocking collectives, per_device(): lax.all_to_all(pieces.reshape(holders, 1, PIECE * LANES), 'sp', split_axi...  51.9 us
    all_to_all x1, blocking collectives, per_device(): lax.all_to_all(packed.reshape(owners, MESSAGE, LANES), 'ev', split_axis=0...  15.2 us
    pallas_call x1, Pallas kernels, per_device(): pl.pallas_call(diffuse_kernel, out_shape=jax.ShapeDtypeStruct((mine, rows...  2.04 us

profile of v5, /device:TPU:8, one launch (start us, length us, event | category | flops | bytes accessed | tf_op | source)
XLA Modules:
  0.0 71.2 jit_solution(17410100597249007342)
XLA Ops:
  0.0 1.3 %shard_map.55 = (f32[576,128]{1,0:T(8,128)S(1)}, f32[3,512,128]{2,1,0:T(8,128)S(1)}, f32[128,128]{1,0:T(8,128)S(1)}, f32[2,8,128]{2,1,0:T(8,128)S(1)}, bf16[256,...) custom-call(s32[1,8]{1,0:T(1,128)} %ids_hbm.1, f32[256,128]{1,0:T(8,128)} %bitcast.7, f32[512,1024]{1,0:T(8,128)} %scale_hbm.1, ...), custom_call_target="tpu_custom_call" | custom-call | tf_op jit(solution)/shard_map/pallas_call | solution.py:353
  1.4 15.2 %all_to_all.10.arrived_ref = f32[8,72,128]{2,1,0:T(8,128)S(1)} all-to-all(f32[8,72,128]{2,1,0:T(8,128)S(1)} %bitcast.6), channel_id=1, replica_groups=mesh['ev'=8,'sp'=64] {'ev'}, dimensions={0} | all-to-all | bytes 589824 | tf_op jit(solution)/shard_map/all_to_all | solution.py:379
  16.5 0.8 %shard_map.56 = (f32[1088,128]{1,0:T(8,128)S(1)}, f32[128,128]{1,0:T(8,128)S(1)}) custom-call(f32[8,72,128]{2,1,0:T(8,128)S(1)} %all_to_all.10.arrived_ref, f32[3,512,128]{2,1,0:T(8,128)S(1)} %get-tuple-element.14.scale_ref, f32[128,128]{1,0:T(8,128)S(1)} %get-tuple-element.15.smoother_ref), custom_call_target="tpu_custom_call" | custom-call | tf_op jit(solution)/shard_map/pallas_call | solution.py:382
  17.3 51.9 %all_to_all.11 = f32[64,1,2176]{2,1,0:T(1,128)S(1)} all-to-all(f32[64,1,2176]{2,1,0:T(1,128)S(1)} %bitcast.5), channel_id=1, replica_groups=mesh['ev'=8,'sp'=64] {'sp'}, dimensions={0} | all-to-all | bytes 1114112 | tf_op jit(solution)/shard_map/all_to_all | solution.py:396
  69.2 2.0 %shard_map.57 = f32[2,512,128]{2,1,0:T(8,128)} custom-call(f32[1088,128]{1,0:T(8,128)S(1)} %bitcast.4, f32[2,8,128]{2,1,0:T(8,128)S(1)} %get-tuple-element.17.factor_ref, f32[3,512,128]{2,1,0:T(8,128)S(1)} %get-tuple-element.14.scale_ref, f32[128,128]{1,0:T(8,128)S(1)} %get-tuple-element.18.side_scale_ref, bf16[256,128]{1,0:T(8,128)(2,1)S(1)} %get-tuple-element.19.near_ref, ...), custom_call_target="tpu_custom_call" | custom-call | tf_op jit(solution)/shard_map/pallas_call | solution.py:402
